TPU v7x, 32 devices: a whole 2x2x4 slice. The times are simulated.
32 devices in a mesh: fsdp: 8 (over y, x, core), seq: 4 (over z).
Axes of the slice: x: 2, y: 2, z: 4, core: 2. Of those that a mesh axis runs over, the one named last changes fastest.
Arguments:
- hidden_in: bfloat16 [8, 1024, 2048], P('fsdp', 'seq'), may hold values from -6 to 6
- lengths: int32 [8], P('fsdp'), may hold values from 512 to 1024, as said below
- cotangent: bfloat16 [8, 1024, 2048], P('fsdp', 'seq'), may hold values from -6 to 6
- in_weight: bfloat16 [2048, 6144], P(('fsdp', 'seq')), may hold values from -0.125 to 0.125
- in_bias: bfloat16 [6144], P(('fsdp', 'seq')), may hold values from -0.29882812 to 0.29882812
- out_weight: bfloat16 [2048, 2048], P(('fsdp', 'seq')), may hold values from -1 to 1
- out_bias: bfloat16 [2048], P(('fsdp', 'seq')), may hold values from -2 to 2
- up_weight: bfloat16 [8192, 2048], P(('fsdp', 'seq')), may hold values from -0.125 to 0.125
- up_bias: bfloat16 [8192], P(('fsdp', 'seq')), may hold values from -2 to 2
- down_weight: bfloat16 [8192, 2048], P(('fsdp', 'seq')), may hold values from -0.0625 to 0.0625
- down_bias: bfloat16 [2048], P(('fsdp', 'seq')), may hold values from -2 to 2
- first_gain: bfloat16 [2048], P(('fsdp', 'seq')), may hold values from 0.5 to 1.5
- first_shift: bfloat16 [2048], P(('fsdp', 'seq')), may hold values from -2 to 2
- second_gain: bfloat16 [2048], P(('fsdp', 'seq')), may hold values from 0.5 to 1.5
- second_shift: bfloat16 [2048], P(('fsdp', 'seq')), may hold values from -2 to 2
Outputs:
- layer_output: float32 [8, 1024, 2048], P('fsdp', 'seq')
- input_gradient: float32 [8, 1024, 2048], P('fsdp', 'seq')
- in_weight_gradient: float32 [2048, 6144], P(('fsdp', 'seq'))
- in_bias_gradient: float32 [6144], P(('fsdp', 'seq'))
- out_weight_gradient: float32 [2048, 2048], P(('fsdp', 'seq'))
- out_bias_gradient: float32 [2048], P(('fsdp', 'seq'))
- up_weight_gradient: float32 [8192, 2048], P(('fsdp', 'seq'))
- up_bias_gradient: float32 [8192], P(('fsdp', 'seq'))
- down_weight_gradient: float32 [8192, 2048], P(('fsdp', 'seq'))
- down_bias_gradient: float32 [2048], P(('fsdp', 'seq'))
- first_gain_gradient: float32 [2048], P(('fsdp', 'seq'))
- first_shift_gradient: float32 [2048], P(('fsdp', 'seq'))
- second_gain_gradient: float32 [2048], P(('fsdp', 'seq'))
- second_shift_gradient: float32 [2048], P(('fsdp', 'seq'))
Inputs may be any that keep to these rules, and one draw needn't show every extreme that they name: `lengths`: tokens in use at the front of each slot; in every draw one slot is full and one holds 512 tokens.
All inputs are finite; a program needn't handle non-finite values.
Results may differ from a plain program's by a relative error of at most 0.014.
Values may be sent and summed in bfloat16 or wider, within the bound.
No kernel may reach another device: no remote copies, remote signals or barrier semaphores. Data moves between devices by JAX's collectives and lax.ppermute only.
A program may use at most 384 MiB of HBM per device.

v0:
```python
import jax
import jax.numpy as jnp
from jax import lax
from jax.sharding import PartitionSpec as P

HEADS = 16
HEAD_DIM = 128
ROT = 32


EPSILON = 1e-05
MASKED_SCORE = -1e30


def layer_norm(values, norm_gain, norm_shift):
    centred = values - jnp.mean(values, axis=-1, keepdims=True)
    spread = jnp.mean(centred * centred, axis=-1, keepdims=True)
    return centred * lax.rsqrt(spread + EPSILON) * norm_gain + norm_shift


def rotary_tables(positions):
    halves = jnp.arange(ROT // 2, dtype=jnp.float32)
    frequency = 1.0 / 10000.0 ** (halves * 2.0 / ROT)
    angles = positions.astype(jnp.float32)[:, None] * frequency[None, :]
    angles = jnp.concatenate([angles, angles], axis=1)
    return (jnp.cos(angles), jnp.sin(angles))


def rotate(values, cosine_table, sine_table):
    leading = values[..., :ROT]
    middle = ROT // 2
    turned = jnp.concatenate([-leading[..., middle:], leading[..., :middle]], axis=-1)
    leading = leading * cosine_table[:, None, :] + turned * sine_table[:, None, :]
    return jnp.concatenate([leading, values[..., ROT:]], axis=-1)


def exact_gelu(values):
    return jax.nn.gelu(values, approximate=False)


def matmul(left_side, right_side):
    return jnp.dot(left_side, right_side, preferred_element_type=jnp.float32)


def times_transposed(left_side, right_side):
    return lax.dot_general(
        left_side, right_side, (((1,), (1,)), ((), ())), preferred_element_type=jnp.float32
    )


def transposed_times(left_side, right_side):
    return lax.dot_general(
        left_side, right_side, (((0,), (0,)), ((), ())), preferred_element_type=jnp.float32
    )


def attend_slot(query, key_rows, value_rows, keep_mask):
    length_full = query.shape[0]
    block_rows = min(512, length_full)
    block_count = length_full // block_rows
    columns = jnp.arange(length_full, dtype=jnp.int32)
    scale_factor = HEAD_DIM ** (-0.5)

    def one_block(first_row):
        row_index = first_row + jnp.arange(block_rows, dtype=jnp.int32)
        query_block = lax.dynamic_slice_in_dim(query, first_row, block_rows, 0)
        scores = (
            jnp.einsum("qhd,khd->hqk", query_block, key_rows, preferred_element_type=jnp.float32)
            * scale_factor
        )
        allowed = (columns[None, :] <= row_index[:, None]) & keep_mask[None, :]
        scores = jnp.where(allowed[None], scores, MASKED_SCORE)
        largest = jnp.max(scores, axis=-1, keepdims=True)
        weights = jnp.exp(scores - largest)
        totals = jnp.sum(weights, axis=-1, keepdims=True)
        probabilities = (weights / totals).astype(jnp.bfloat16)
        mixed = jnp.einsum(
            "hqk,khd->qhd", probabilities, value_rows, preferred_element_type=jnp.float32
        )
        return (mixed, (largest + jnp.log(totals))[..., 0])

    starts = jnp.arange(block_count, dtype=jnp.int32) * block_rows
    mixed, log_sums = lax.map(one_block, starts)
    return (mixed.reshape(length_full, query.shape[1], query.shape[2]), log_sums)


def attend_slot_back(query, key_rows, value_rows, keep_mask, log_sums, mixed_delta):
    length_full = query.shape[0]
    block_rows = min(512, length_full)
    block_count = length_full // block_rows
    columns = jnp.arange(length_full, dtype=jnp.int32)
    scale_factor = HEAD_DIM ** (-0.5)

    def one_block(carried, member):
        key_delta, value_delta = carried
        first_row, log_block = member
        row_index = first_row + jnp.arange(block_rows, dtype=jnp.int32)
        query_block = lax.dynamic_slice_in_dim(query, first_row, block_rows, 0)
        delta_block = lax.dynamic_slice_in_dim(mixed_delta, first_row, block_rows, 0)
        scores = (
            jnp.einsum("qhd,khd->hqk", query_block, key_rows, preferred_element_type=jnp.float32)
            * scale_factor
        )
        allowed = (columns[None, :] <= row_index[:, None]) & keep_mask[None, :]
        scores = jnp.where(allowed[None], scores, MASKED_SCORE)
        probabilities = jnp.where(allowed[None], jnp.exp(scores - log_block[..., None]), 0.0)
        prob_delta = jnp.einsum(
            "qhd,khd->hqk", delta_block, value_rows, preferred_element_type=jnp.float32
        )
        row_dot = jnp.sum(probabilities * prob_delta, axis=-1, keepdims=True)
        score_delta = (probabilities * (prob_delta - row_dot)).astype(jnp.bfloat16)
        query_delta = (
            jnp.einsum("hqk,khd->qhd", score_delta, key_rows, preferred_element_type=jnp.float32)
            * scale_factor
        )
        key_delta = (
            key_delta
            + jnp.einsum(
                "hqk,qhd->khd", score_delta, query_block, preferred_element_type=jnp.float32
            )
            * scale_factor
        )
        value_delta = value_delta + jnp.einsum(
            "hqk,qhd->khd",
            probabilities.astype(jnp.bfloat16),
            delta_block,
            preferred_element_type=jnp.float32,
        )
        return ((key_delta, value_delta), query_delta)

    starts = jnp.arange(block_count, dtype=jnp.int32) * block_rows
    zeroes = jnp.zeros(query.shape, jnp.float32)
    (key_delta, value_delta), query_delta = lax.scan(
        one_block, (zeroes, zeroes), (starts, log_sums)
    )
    return (query_delta.reshape(query.shape), key_delta, value_delta)


def feed_forward(inner_in, up_matrix, up_offset, down_matrix):
    hidden_pre = times_transposed(inner_in, up_matrix) + up_offset.astype(jnp.float32)
    hidden_act, pull_act = jax.vjp(exact_gelu, hidden_pre)
    hidden_low = hidden_act.astype(jnp.bfloat16)
    return (hidden_low, pull_act, matmul(hidden_low, down_matrix))


def feed_back(inner_in, hidden_low, pull_act, delta_rows, up_matrix, down_matrix):
    delta_down = transposed_times(hidden_low, delta_rows)
    delta_pre = pull_act(times_transposed(delta_rows, down_matrix))[0].astype(jnp.bfloat16)
    delta_up = transposed_times(delta_pre, inner_in)
    delta_up_bias = jnp.sum(delta_pre.astype(jnp.float32), axis=0)
    delta_inner = matmul(delta_pre, up_matrix)
    return (delta_up, delta_up_bias, delta_down, delta_inner)


def local(
    hidden_in,
    lengths,
    cotangent,
    in_weight,
    in_bias,
    out_weight,
    out_bias,
    up_weight,
    up_bias,
    down_weight,
    down_bias,
    first_gain,
    first_shift,
    second_gain,
    second_shift,
):
    slot_count, token_count, width = hidden_in.shape
    seq_count = lax.axis_size("seq")
    seq_index = lax.axis_index("seq")
    length_full = token_count * seq_count
    row_count = slot_count * token_count
    (
        in_matrix,
        in_offset,
        out_matrix,
        out_offset,
        gain_one,
        shift_one,
        gain_two,
        shift_two,
        down_offset,
    ) = (
        lax.all_gather(in_weight, ("fsdp", "seq"), axis=0, tiled=True),
        lax.all_gather(in_bias, ("fsdp", "seq"), axis=0, tiled=True),
        lax.all_gather(out_weight, ("fsdp", "seq"), axis=0, tiled=True),
        lax.all_gather(out_bias, ("fsdp", "seq"), axis=0, tiled=True),
        lax.all_gather(first_gain, ("fsdp", "seq"), axis=0, tiled=True),
        lax.all_gather(first_shift, ("fsdp", "seq"), axis=0, tiled=True),
        lax.all_gather(second_gain, ("fsdp", "seq"), axis=0, tiled=True),
        lax.all_gather(second_shift, ("fsdp", "seq"), axis=0, tiled=True),
        lax.all_gather(down_bias, ("fsdp", "seq"), axis=0, tiled=True),
    )
    positions = seq_index * token_count + jnp.arange(token_count, dtype=jnp.int32)
    keep_local = positions[None, :] < lengths[:, None]
    keep_full = jnp.arange(length_full, dtype=jnp.int32)[None, :] < lengths[:, None]
    source = hidden_in.astype(jnp.float32)
    normed_one, pull_one = jax.vjp(
        layer_norm, source, gain_one.astype(jnp.float32), shift_one.astype(jnp.float32)
    )
    first_in = normed_one.astype(jnp.bfloat16).reshape(row_count, width)
    cosine_table, sine_table = rotary_tables(positions)
    joined = matmul(first_in, in_matrix) + in_offset.astype(jnp.float32)
    joined = joined.reshape(slot_count, token_count, 3, HEADS, HEAD_DIM)

    def rotate_both(query_part, key_part):
        return (
            rotate(query_part, cosine_table, sine_table),
            rotate(key_part, cosine_table, sine_table),
        )

    turned, pull_turn = jax.vjp(rotate_both, joined[:, :, 0], joined[:, :, 1])
    query, key_rows, value_rows = (
        lax.all_to_all(
            turned[0].astype(jnp.bfloat16), "seq", split_axis=2, concat_axis=1, tiled=True
        ),
        lax.all_to_all(
            turned[1].astype(jnp.bfloat16), "seq", split_axis=2, concat_axis=1, tiled=True
        ),
        lax.all_to_all(
            joined[:, :, 2].astype(jnp.bfloat16), "seq", split_axis=2, concat_axis=1, tiled=True
        ),
    )
    mixed_heads, log_sums = jax.vmap(attend_slot)(query, key_rows, value_rows, keep_full)
    mixed = lax.all_to_all(
        mixed_heads.astype(jnp.bfloat16), "seq", split_axis=1, concat_axis=2, tiled=True
    ).reshape(row_count, width)
    attn_branch = matmul(mixed, out_matrix) + out_offset.astype(jnp.float32)
    normed_two, pull_two = jax.vjp(
        layer_norm, source, gain_two.astype(jnp.float32), shift_two.astype(jnp.float32)
    )
    second_in = normed_two.astype(jnp.bfloat16)
    delta_out = jnp.where(keep_local[..., None], cotangent.astype(jnp.float32), 0.0)
    delta_low = delta_out.astype(jnp.bfloat16)
    delta_rows = delta_low.reshape(row_count, width)
    up_matrix, up_offset, down_matrix = (
        lax.all_gather(up_weight, "fsdp", axis=0, tiled=True),
        lax.all_gather(up_bias, "fsdp", axis=0, tiled=True),
        lax.all_gather(down_weight, "fsdp", axis=0, tiled=True),
    )
    inner_in = lax.all_gather(second_in, "seq", axis=1, tiled=True).reshape(
        slot_count * length_full, width
    )
    hidden_low, pull_act, branch_part = feed_forward(inner_in, up_matrix, up_offset, down_matrix)
    branch_sum = lax.psum_scatter(
        branch_part.reshape(slot_count, length_full, width).astype(jnp.bfloat16),
        "seq",
        scatter_dimension=1,
        tiled=True,
    ).astype(jnp.float32)
    mlp_branch = branch_sum + down_offset.astype(jnp.float32)
    delta_all = lax.all_gather(delta_low, "seq", axis=1, tiled=True).reshape(
        slot_count * length_full, width
    )
    delta_up, delta_up_bias, delta_down, delta_inner = feed_back(
        inner_in, hidden_low, pull_act, delta_all, up_matrix, down_matrix
    )
    second_delta = lax.psum_scatter(
        delta_inner.reshape(slot_count, length_full, width).astype(jnp.bfloat16),
        "seq",
        scatter_dimension=1,
        tiled=True,
    ).astype(jnp.float32)
    up_gradient, up_bias_gradient, down_gradient = (
        lax.psum_scatter(
            delta_up.astype(jnp.bfloat16), "fsdp", scatter_dimension=0, tiled=True
        ).astype(jnp.float32),
        lax.psum_scatter(
            delta_up_bias.astype(jnp.bfloat16), "fsdp", scatter_dimension=0, tiled=True
        ).astype(jnp.float32),
        lax.psum_scatter(
            delta_down.astype(jnp.bfloat16), "fsdp", scatter_dimension=0, tiled=True
        ).astype(jnp.float32),
    )
    layer_output = jnp.where(
        keep_local[..., None],
        source + attn_branch.reshape(slot_count, token_count, width) + mlp_branch,
        0.0,
    )
    source_two, gain_two_delta, shift_two_delta = pull_two(second_delta)
    bias_sum = jnp.sum(delta_out.reshape(row_count, width), axis=0)
    out_delta = transposed_times(mixed, delta_rows)
    mixed_delta = times_transposed(delta_rows, out_matrix).astype(jnp.bfloat16)
    mixed_delta = lax.all_to_all(
        mixed_delta.reshape(slot_count, token_count, HEADS, HEAD_DIM),
        "seq",
        split_axis=2,
        concat_axis=1,
        tiled=True,
    )
    query_delta, key_delta, value_delta = jax.vmap(attend_slot_back)(
        query, key_rows, value_rows, keep_full, log_sums, mixed_delta
    )
    query_back, key_back, value_back = (
        lax.all_to_all(
            query_delta.astype(jnp.bfloat16), "seq", split_axis=1, concat_axis=2, tiled=True
        ),
        lax.all_to_all(
            key_delta.astype(jnp.bfloat16), "seq", split_axis=1, concat_axis=2, tiled=True
        ),
        lax.all_to_all(
            value_delta.astype(jnp.bfloat16), "seq", split_axis=1, concat_axis=2, tiled=True
        ),
    )
    query_plain, key_plain = pull_turn(
        (query_back.astype(jnp.float32), key_back.astype(jnp.float32))
    )
    joined_delta = jnp.stack([query_plain, key_plain, value_back.astype(jnp.float32)], axis=2)
    joined_delta = joined_delta.reshape(row_count, 3 * width).astype(jnp.bfloat16)
    in_delta = transposed_times(first_in, joined_delta)
    in_bias_delta = jnp.sum(joined_delta.astype(jnp.float32), axis=0)
    first_delta = times_transposed(joined_delta, in_matrix).reshape(slot_count, token_count, width)
    source_one, gain_one_delta, shift_one_delta = pull_one(first_delta)
    (
        in_gradient,
        in_bias_gradient,
        out_gradient,
        bias_gradient,
        gain_one_gradient,
        shift_one_gradient,
        gain_two_gradient,
        shift_two_gradient,
    ) = (
        lax.psum_scatter(in_delta, ("fsdp", "seq"), scatter_dimension=0, tiled=True),
        lax.psum_scatter(in_bias_delta, ("fsdp", "seq"), scatter_dimension=0, tiled=True),
        lax.psum_scatter(out_delta, ("fsdp", "seq"), scatter_dimension=0, tiled=True),
        lax.psum_scatter(bias_sum, ("fsdp", "seq"), scatter_dimension=0, tiled=True),
        lax.psum_scatter(gain_one_delta, ("fsdp", "seq"), scatter_dimension=0, tiled=True),
        lax.psum_scatter(shift_one_delta, ("fsdp", "seq"), scatter_dimension=0, tiled=True),
        lax.psum_scatter(gain_two_delta, ("fsdp", "seq"), scatter_dimension=0, tiled=True),
        lax.psum_scatter(shift_two_delta, ("fsdp", "seq"), scatter_dimension=0, tiled=True),
    )
    input_gradient = delta_out + source_one + source_two
    return (
        layer_output,
        input_gradient,
        in_gradient,
        in_bias_gradient,
        out_gradient,
        bias_gradient,
        up_gradient,
        up_bias_gradient,
        down_gradient,
        bias_gradient,
        gain_one_gradient,
        shift_one_gradient,
        gain_two_gradient,
        shift_two_gradient,
    )


def solution(mesh):
    return jax.shard_map(
        local,
        mesh=mesh,
        in_specs=(
            P("fsdp", "seq", None),
            P("fsdp"),
            P("fsdp", "seq", None),
            P(("fsdp", "seq"), None),
            P(("fsdp", "seq")),
            P(("fsdp", "seq"), None),
            P(("fsdp", "seq")),
            P(("fsdp", "seq"), None),
            P(("fsdp", "seq")),
            P(("fsdp", "seq"), None),
            P(("fsdp", "seq")),
            P(("fsdp", "seq")),
            P(("fsdp", "seq")),
            P(("fsdp", "seq")),
            P(("fsdp", "seq")),
        ),
        out_specs=(
            P("fsdp", "seq", None),
            P("fsdp", "seq", None),
            P(("fsdp", "seq"), None),
            P(("fsdp", "seq")),
            P(("fsdp", "seq"), None),
            P(("fsdp", "seq")),
            P(("fsdp", "seq"), None),
            P(("fsdp", "seq")),
            P(("fsdp", "seq"), None),
            P(("fsdp", "seq")),
            P(("fsdp", "seq")),
            P(("fsdp", "seq")),
            P(("fsdp", "seq")),
            P(("fsdp", "seq")),
        ),
        check_vma=False,
    )
```

profile of v0, /device:TPU:0, one launch (start us, length us, event | category | flops | bytes accessed | tf_op | source)
XLA Modules:
  0.0 1959.6 jit_solution(5670677345125691977)
XLA Ops:
  16.4 43.3 %all-reduce.25 = (bf16[6144]{0:T(1024)(128)(2,1)S(1)}, bf16[2048]{0:T(1024)(128)(2,1)S(1)}, bf16[2048]{0:T(1024)(128)(2,1)S(1)}, bf16[2048]{0:T(1024)(128)(2,1)S...) all-reduce(bf16[6144]{0:T(1024)(128)(2,1)S(1)} %dynamic-update-slic, ...), channel_id=1, replica_groups=mesh['fsdp'=8,'seq'=4] {'fsdp','seq'}, use_global_device_ids=true, to_apply=%add.12 | all-reduce | flops 18432 | bytes 73728
  59.7 2.7 fusion.76
  67.0 10.1 all-gather
  77.1 65.9 %all-gather.12.cloned.1.call-done = bf16[1,1024,2048]{2,1,0:T(8,128)(2,1)} async-done(((bf16[1,256,2048]{2,1,0:T(8,128)(2,1)}), bf16[1,1024,2048]{2,1,0:T(8,128)(2,1)}) %all-gather.12.cloned.1.call-update) | async-done | bytes 4194320 | tf_op jit(solution)/shard_map/all_gather | solution.py:245
  143.0 54.8 %all-gather.14.cloned.1.call-done = bf16[2048,2048]{1,0:T(8,128)(2,1)} async-done(((bf16[256,2048]{1,0:T(8,128)(2,1)}), bf16[2048,2048]{1,0:T(8,128)(2,1)}) %all-gather.14.cloned.1.call-update) | async-done | bytes 8388624 | tf_op jit(solution)/shard_map/all_gather | solution.py:241
  197.9 31.6 %multiply_convert_fusion.1 = (bf16[1024,2048]{1,0:T(8,128)(2,1)}, f32[1024,2048]{1,0:T(8,128)}, f32[1024,2048]{1,0:T(8,128)}) fusion(f32[2048]{0:T(1024)S(1)} %bitcast.299, bf16[2048,2048]{1,0:T(8,128)(2,1)} %all-gather.14.cloned.1.call-done, bf16[1,1024,2048]{2,1,0:T(8,128)(2,1)} %all-gather.12.cloned.1.call-done), kind=kOutput, calls=%fused_computation.61 | convolution fusion | flops 8728346624 | bytes 33562624 | tf_op jit(solution)/shard_map/dot_general | solution.py:46
  229.5 50.8 %all-gather.18.cloned.1.call-done = bf16[1,1024,2048]{2,1,0:T(8,128)(2,1)} async-done(((bf16[1,256,2048]{2,1,0:T(8,128)(2,1)}), bf16[1,1024,2048]{2,1,0:T(8,128)(2,1)}) %all-gather.18.cloned.1.call-update) | async-done | bytes 4194320 | tf_op jit(solution)/shard_map/all_gather | solution.py:256
  280.3 54.7 %all-gather.16.cloned.1.call-done = bf16[2048,2048]{1,0:T(8,128)(2,1)} async-done(((bf16[256,2048]{1,0:T(8,128)(2,1)}), bf16[2048,2048]{1,0:T(8,128)(2,1)}) %all-gather.16.cloned.1.call-update) | async-done | bytes 8388624 | tf_op jit(solution)/shard_map/all_gather | solution.py:243
  335.0 19.4 fusion.110
  356.3 12.8 convert_bitcast_fusion
  369.2 14.1 convolution_convert_fusion.1
  383.8 31.3 %all-gather.10.cloned.1.call-done = bf16[2048,2048]{1,0:T(8,128)(2,1)} async-done(((bf16[64,2048]{1,0:T(8,128)(2,1)}), bf16[2048,2048]{1,0:T(8,128)(2,1)}) %all-gather.10.cloned.1.call-update) | async-done | bytes 8388624 | tf_op jit(solution)/shard_map/all_gather | solution.py:190
  415.2 5.7 fusion.88
  422.4 4.5 all-to-all-start.4
  426.9 163.8 %all-gather.8.cloned.1.call-done = bf16[2048,6144]{1,0:T(8,128)(2,1)} async-done(((bf16[64,6144]{1,0:T(8,128)(2,1)}), bf16[2048,6144]{1,0:T(8,128)(2,1)}) %all-gather.8.cloned.1.call-update) | async-done | bytes 25165840 | tf_op jit(solution)/shard_map/all_gather | solution.py:188
  590.8 12.5 fusion.68
  613.0 4.2 all-to-all-start.1
  619.2 53.1 %all-to-all-done.1 = bf16[1,256,16,128]{3,1,0,2:T(8,128)(2,1)} async-done(((bf16[1,256,16,128]{3,1,0,2:T(8,128)(2,1)}), bf16[1,256,16,128]{3,1,0,2:T(8,128)(2,1)}, u32[]{:S(2)}, u32[]{:S(2)}) %all-to-all-start.1) | async-done | bytes 1048608 | tf_op jit(solution)/shard_map/all_to_all | solution.py:221
  672.3 3.9 all-to-all-start
  679.2 33.3 %all-to-all-done = bf16[1,256,16,128]{3,1,0,2:T(8,128)(2,1)S(1)} async-done(((bf16[1,256,16,128]{3,1,0,2:T(8,128)(2,1)}), bf16[1,256,16,128]{3,1,0,2:T(8,128)(2,1)S(1)}, u32[]{:S(2)}, u32[]{:S(2)}) %all-to-all-start) | async-done | bytes 1048608 | tf_op jit(solution)/shard_map/all_to_all | solution.py:218
  712.5 4.3 all-to-all-start.2
  716.8 15.2 convolution_convert_fusion
  736.8 5.4 all-to-all-done.2
  745.7 26.7 %while.31 = (s32[]{:T(128)}, bf16[2,1,512,4,128]{4,2,0,3,1:T(8,128)(2,1)}, f32[2,1,4,512]{3,2,1,0:T(4,128)S(1)}, s32[2]{0:T(128)S(1)}, bf16[1,1024,4,128]{3,1,2,...) while((s32[]{:T(128)}, ...), condition=%wide.region_5.6_spmd.clone, body=%wide.region_2.5_spmd.clone.sunk | while | flops 1099955712 | bytes 35199700 | solution.py:83
  750.0 2.9 fusion.147
  755.3 3.7 fusion.149
  763.3 2.9 fusion.147
  768.7 3.7 fusion.149
  773.5 54.9 %while.32 = (s32[]{:T(128)}, f32[1,1024,4,128]{1,3,2,0:T(8,128)S(1)}, f32[1,1024,4,128]{1,3,2,0:T(8,128)}, bf16[2,1,512,4,128]{4,2,0,3,1:T(8,128)(2,1)}, s32[2]{...) while((s32[]{:T(128)}, ...), condition=%wide.region_9.10_spmd.clone, body=%wide.region_7.9_spmd.clone.sunk | while | flops 2709257728 | bytes 170966912 | solution.py:133
  776.2 2.8 fusion.158
  780.8 3.7 multiply_reduce_fusion.2
  784.5 3.3 copy-done
  790.2 3.8 bitcast_add_fusion.4
  802.9 3.0 fusion.158
  807.7 3.7 multiply_reduce_fusion.2
  811.4 3.5 copy-done
  817.3 3.8 bitcast_add_fusion.4
  824.5 3.9 bitcast_add_fusion.5
  828.4 3.1 copy.149
  831.5 3.5 all-to-all-start.5
  836.7 22.4 %all-to-all-done.5 = bf16[1,1024,4,128]{3,2,0,1:T(4,128)(2,1)S(1)} async-done(((bf16[1,1024,4,128]{3,2,0,1:T(4,128)(2,1)}), bf16[1,1024,4,128]{3,2,0,1:T(4,128)(2,1)S(1)}, u32[]{:S(2)}, u32[]{:S(2)}) %all-to-all-start.5) | async-done | bytes 1048608 | tf_op jit(solution)/shard_map/all_to_all | solution.py:299
  860.1 3.5 all-to-all-start.6
  863.7 14.1 convert_bitcast_fusion.1
  877.8 2.9 copy.154
  880.6 8.2 all-to-all-done.6
  888.9 4.3 all-to-all-start.7
  893.2 3.0 copy.143
  900.8 45.5 %all-to-all-done.7 = bf16[1,1024,4,128]{3,2,0,1:T(4,128)(2,1)} async-done(((bf16[1,1024,4,128]{3,2,0,1:T(4,128)(2,1)}), bf16[1,1024,4,128]{3,2,0,1:T(4,128)(2,1)}, u32[]{:S(2)}, u32[]{:S(2)}) %all-to-all-start.7) | async-done | bytes 1048608 | tf_op jit(solution)/shard_map/all_to_all | solution.py:305
  946.3 4.2 all-to-all-start.3
  958.3 3.6 convert_reduce_fusion
  961.9 4.7 copy.156
  966.6 30.5 %all-to-all-done.3 = bf16[1,1024,4,128]{3,2,0,1:T(4,128)(2,1)S(1)} async-done(((bf16[1,1024,4,128]{3,2,0,1:T(4,128)(2,1)}), bf16[1,1024,4,128]{3,2,0,1:T(4,128)(2,1)S(1)}, u32[]{:S(2)}, u32[]{:S(2)}) %all-to-all-start.3) | async-done | bytes 1048608 | tf_op jit(solution)/shard_map/all_to_all | solution.py:229
  999.8 14.7 fusion.79
  1016.9 3.8 fusion.81
  1020.7 3.4 fusion.86
  1024.3 8.1 fusion.94
  1033.1 21.9 %fusion.103 = f32[2048,6144]{1,0:T(8,128)} fusion(bf16[256,6144]{0,1:T(8,128)(2,1)} %bitcast.282, bf16[1,256,2048]{2,1,0:T(8,128)(2,1)S(1)} %copy-done.4, f32[2048]{0:T(1024)S(1)} %copy-done.31, f32[2048]{0:T(1024)S(1)} %copy-done.29, f32[256]{0:T(256)S(1)} %copy-done.35, f32[256]{0:T(256)S(1)} %copy-done.37), kind=kOutput, calls=%fused_computation.179 | convolution fusion | flops 6445596672 | bytes 54544384 | tf_op jit(solution)/shard_map/dot_general | solution.py:52
  1056.9 13.8 all-reduce.19
  1071.3 2.8 convert_element_type.312
  1074.1 2.8 convert_element_type.315
  1076.9 7.5 fusion.71
  1084.4 63.4 %all-reduce.28.cloned.1.call-done = (f32[6144]{0:T(1024)}, f32[2048]{0:T(1024)}, f32[2048]{0:T(1024)}, f32[2048]{0:T(1024)}, f32[2048]{0:T(1024)}, /*index=5*/f32[2048]{0:T(1024)}) async-done(((f32[6144]{0:T(1024)}, f32[2048]{0:T(1024)}, f32[2048]{0:T(1024)}, f32[2048]{0:T(1024)}, f32[2048]{0:T(1024)}, /*index=5*/f32[2048]{0:T(1024)}), (f32[6144]{0:T(1024)}, f32[2048]{0:T(1024)}, f32[2048]{0:T(1024)}, ...) | async-done | bytes 65552
  1155.0 361.0 %reduce-scatter.13.cloned.1.call-done = f32[64,2048]{1,0:T(8,128)} async-done(((f32[2048,2048]{1,0:T(8,128)}), f32[64,2048]{1,0:T(8,128)}) %reduce-scatter.13.cloned.1.call-update) | async-done | bytes 524304 | tf_op jit(solution)/shard_map/reduce_scatter | solution.py:330
  1516.0 436.4 %reduce-scatter.11.cloned.1.call-done = f32[64,6144]{1,0:T(8,128)} async-done(((f32[2048,6144]{1,0:T(8,128)}), f32[64,6144]{1,0:T(8,128)}) %reduce-scatter.11.cloned.1.call-update) | async-done | bytes 1572880 | tf_op jit(solution)/shard_map/reduce_scatter | solution.py:328
  (259 shorter events, 99.9 us)
Async XLA Ops:
  7.2 135.9 %all-gather.12.cloned.1.call-start = ((), (), s32[]{:S(2)}) async-start(), calls=%async_computation.16 | async-start | bytes 5242880 | tf_op jit(solution)/shard_map/all_gather | solution.py:245
  7.2 56.6 %copy-start.18 = (bf16[1,256,2048]{2,1,0:T(8,128)(2,1)S(1)}, bf16[1,256,2048]{2,1,0:T(8,128)(2,1)}, u32[]{:S(2)}) copy-start(bf16[1,256,2048]{2,1,0:T(8,128)(2,1)} %param.21) | copy-start | bytes 3145732
  8.8 582.0 %copy-start.36 = (f32[256]{0:T(256)}, f32[256]{0:T(256)S(1)}, u32[]{:S(2)}) copy-start(f32[256]{0:T(256)S(1)} %broadcast_multiply_fusion.1) | copy-start | bytes 3076
  10.4 49.2 %copy-start.38 = (f32[256]{0:T(256)}, f32[256]{0:T(256)S(1)}, u32[]{:S(2)}) copy-start(f32[256]{0:T(256)S(1)} %fusion.78) | copy-start | bytes 3076
  10.5 580.3 %copy-start.34 = (f32[256]{0:T(256)}, f32[256]{0:T(256)S(1)}, u32[]{:S(2)}) copy-start(f32[256]{0:T(256)S(1)} %fusion.101) | copy-start | bytes 3076
  59.7 5.4 copy-start.32
  62.4 4.6 copy-start.45
  62.4 135.5 %all-gather.14.cloned.1.call-start = ((), (), s32[]{:S(2)}) async-start(), calls=%async_computation.17 | async-start | bytes 9437184 | tf_op jit(solution)/shard_map/all_gather | solution.py:241
  63.1 217.1 %all-gather.18.cloned.1.call-start = ((), (), s32[]{:S(2)}) async-start(), calls=%async_computation.20 | async-start | bytes 5242880 | tf_op jit(solution)/shard_map/all_gather | solution.py:256
  63.9 3.1 copy-start.40
  65.1 269.8 %all-gather.16.cloned.1.call-start = ((), (), s32[]{:S(2)}) async-start(), calls=%async_computation.18 | async-start | bytes 9437184 | tf_op jit(solution)/shard_map/all_gather | solution.py:243
  65.7 349.4 %all-gather.10.cloned.1.call-start = ((), (), s32[]{:S(2)}) async-start(), calls=%async_computation.15 | async-start | bytes 8650752 | tf_op jit(solution)/shard_map/all_gather | solution.py:190
  66.3 524.4 %all-gather.8.cloned.1.call-start = ((), (), s32[]{:S(2)}) async-start(), calls=%async_computation.14 | async-start | bytes 25952256 | tf_op jit(solution)/shard_map/all_gather | solution.py:188
  66.9 932.8 %reduce-scatter.9.cloned.1.call-start = ((), (), s32[]{:S(2)}) async-start(), calls=%async_computation.21 | async-start | bytes 5242880 | tf_op jit(solution)/shard_map/reduce_scatter | solution.py:262
  369.2 702.1 %reduce-scatter.15.cloned.1.call-start = ((), (), s32[]{:S(2)}) async-start(), calls=%async_computation.24 | async-start | bytes 9437184 | tf_op jit(solution)/shard_map/reduce_scatter | solution.py:269
  383.4 31.8 %copy-start.12 = (bf16[1,256,2048]{2,1,0:T(8,128)(2,1)S(1)}, bf16[1,256,2048]{2,1,0:T(8,128)(2,1)}, u32[]{:S(2)}) copy-start(bf16[1,256,2048]{2,1,0:T(8,128)(2,1)} %fusion.87) | copy-start | bytes 3145732
  383.4 207.4 %copy-start.28 = (f32[2048]{0:T(1024)}, f32[2048]{0:T(1024)S(1)}, u32[]{:S(2)}) copy-start(f32[2048]{0:T(1024)S(1)} %convert_element_type.269) | copy-start | bytes 24580
  383.4 207.4 %copy-start.30 = (f32[2048]{0:T(1024)}, f32[2048]{0:T(1024)S(1)}, u32[]{:S(2)}) copy-start(f32[2048]{0:T(1024)S(1)} %convert_element_type.270) | copy-start | bytes 24580
  383.7 226.4 %copy-start.24 = (f32[256,32]{1,0:T(8,128)}, f32[256,32]{1,0:T(8,128)S(1)}, u32[]{:S(2)}) copy-start(f32[256,32]{1,0:T(8,128)S(1)} %copy.133) | copy-start | bytes 98308
  383.8 226.3 %copy-start.26 = (f32[256,32]{1,0:T(8,128)}, f32[256,32]{1,0:T(8,128)S(1)}, u32[]{:S(2)}) copy-start(f32[256,32]{1,0:T(8,128)S(1)} %copy.134) | copy-start | bytes 98308
  420.9 169.9 %copy-start.3 = (bf16[1,256,2048]{2,1,0:T(8,128)(2,1)S(1)}, bf16[1,256,2048]{2,1,0:T(8,128)(2,1)}, u32[]{:S(2)}) copy-start(bf16[1,256,2048]{2,1,0:T(8,128)(2,1)} %param.19) | copy-start | bytes 3145732
  422.4 190.6 %all-to-all-start.4 = ((bf16[1,256,16,128]{3,1,0,2:T(8,128)(2,1)}), bf16[1,256,16,128]{3,1,0,2:T(8,128)(2,1)}, u32[]{:S(2)}, u32[]{:S(2)}) async-start(bf16[1,256,16,128]{3,1,0,2:T(8,128)(2,1)} %copy.146), calls=%async_computation.5 | async-start | bytes 2097152 | tf_op jit(solution)/shard_map/all_to_all | solution.py:288
  604.5 2.6 copy-start.10
  613.0 59.3 %all-to-all-start.1 = ((bf16[1,256,16,128]{3,1,0,2:T(8,128)(2,1)}), bf16[1,256,16,128]{3,1,0,2:T(8,128)(2,1)}, u32[]{:S(2)}, u32[]{:S(2)}) async-start(bf16[1,256,16,128]{3,1,0,2:T(8,128)(2,1)} %maximum_bitcast_fusion.1), calls=%async_computation.1 | async-start | bytes 2097152 | tf_op jit(solution)/shard_map/all_to_all | solution.py:221
  672.3 40.2 %all-to-all-start = ((bf16[1,256,16,128]{3,1,0,2:T(8,128)(2,1)}), bf16[1,256,16,128]{3,1,0,2:T(8,128)(2,1)S(1)}, u32[]{:S(2)}, u32[]{:S(2)}) async-start(bf16[1,256,16,128]{3,1,0,2:T(8,128)(2,1)} %maximum_bitcast_fusion), calls=%async_computation | async-start | bytes 2097152 | tf_op jit(solution)/shard_map/all_to_all | solution.py:218
  712.5 19.5 copy-start.22
  712.5 29.8 %all-to-all-start.2 = ((bf16[1,256,16,128]{3,1,0,2:T(8,128)(2,1)}), bf16[1,256,16,128]{3,1,0,2:T(8,128)(2,1)}, u32[]{:S(2)}, u32[]{:S(2)}) async-start(bf16[1,256,16,128]{3,1,0,2:T(8,128)(2,1)} %bitcast.288), calls=%async_computation.2 | async-start | bytes 2097152 | tf_op jit(solution)/shard_map/all_to_all | solution.py:224
  716.8 357.3 %reduce-scatter.17.cloned.1.call-start = ((), (), s32[]{:S(2)}) async-start(), calls=%async_computation.25 | async-start | bytes 9437184 | tf_op jit(solution)/shard_map/reduce_scatter | solution.py:275
  732.1 3.7 copy-start.23
  752.9 2.4 copy-start.5
  766.2 2.4 copy-start.5
  776.2 4.6 copy-start.7
  784.5 3.3 copy-start
  790.2 3.9 copy-start.2
  790.2 7.4 copy-start.1
  794.0 4.1 copy-start.6
  802.9 4.8 copy-start.7
  811.4 3.5 copy-start
  817.3 3.9 copy-start.2
  817.3 6.7 copy-start.1
  821.2 3.3 copy-start.6
  831.5 27.6 %all-to-all-start.5 = ((bf16[1,1024,4,128]{3,2,0,1:T(4,128)(2,1)}), bf16[1,1024,4,128]{3,2,0,1:T(4,128)(2,1)S(1)}, u32[]{:S(2)}, u32[]{:S(2)}) async-start(bf16[1,1024,4,128]{3,2,0,1:T(4,128)(2,1)} %copy.149), calls=%async_computation.6 | async-start | bytes 2097152 | tf_op jit(solution)/shard_map/all_to_all | solution.py:299
  860.1 28.8 %all-to-all-start.6 = ((bf16[1,1024,4,128]{3,2,0,1:T(4,128)(2,1)}), bf16[1,1024,4,128]{3,2,0,1:T(4,128)(2,1)S(1)}, u32[]{:S(2)}, u32[]{:S(2)}) async-start(bf16[1,1024,4,128]{3,2,0,1:T(4,128)(2,1)} %copy.152), calls=%async_computation.7 | async-start | bytes 2097152 | tf_op jit(solution)/shard_map/all_to_all | solution.py:302
  863.6 213.3 %reduce-scatter.7.cloned.1.call-start = ((), (), s32[]{:S(2)}) async-start(), calls=%async_computation.19 | async-start | bytes 5242880 | tf_op jit(solution)/shard_map/reduce_scatter | solution.py:249
  877.8 18.4 copy-start.21
  888.9 57.4 %all-to-all-start.7 = ((bf16[1,1024,4,128]{3,2,0,1:T(4,128)(2,1)}), bf16[1,1024,4,128]{3,2,0,1:T(4,128)(2,1)}, u32[]{:S(2)}, u32[]{:S(2)}) async-start(bf16[1,1024,4,128]{3,2,0,1:T(4,128)(2,1)} %copy.154), calls=%async_computation.8 | async-start | bytes 2097152 | tf_op jit(solution)/shard_map/all_to_all | solution.py:305
  900.8 51.2 %copy-start.27 = (f32[256,32]{1,0:T(8,128)S(1)}, f32[256,32]{1,0:T(8,128)}, u32[]{:S(2)}) copy-start(f32[256,32]{1,0:T(8,128)} %copy-done.26) | copy-start | bytes 98308
  946.3 50.8 %all-to-all-start.3 = ((bf16[1,1024,4,128]{3,2,0,1:T(4,128)(2,1)}), bf16[1,1024,4,128]{3,2,0,1:T(4,128)(2,1)S(1)}, u32[]{:S(2)}, u32[]{:S(2)}) async-start(bf16[1,1024,4,128]{3,2,0,1:T(4,128)(2,1)} %copy.143), calls=%async_computation.3 | async-start | bytes 2097152 | tf_op jit(solution)/shard_map/all_to_all | solution.py:229
  950.5 197.4 %all-reduce.28.cloned.1.call-start = ((), (), s32[]{:S(2)}) async-start(), calls=%async_computation.26 | async-start | bytes 131072
  966.6 33.1 %copy-start.4 = (bf16[1,256,2048]{2,1,0:T(8,128)(2,1)S(1)}, bf16[1,256,2048]{2,1,0:T(8,128)(2,1)}, u32[]{:S(2)}) copy-start(bf16[1,256,2048]{2,1,0:T(8,128)(2,1)} %param.19) | copy-start | bytes 3145732
  966.6 33.1 %copy-start.29 = (f32[2048]{0:T(1024)S(1)}, f32[2048]{0:T(1024)}, u32[]{:S(2)}) copy-start(f32[2048]{0:T(1024)} %copy-done.28) | copy-start | bytes 24580
  966.6 33.1 %copy-start.33 = (f32[2048]{0:T(1024)S(1)}, f32[2048]{0:T(1024)}, u32[]{:S(2)}) copy-start(f32[2048]{0:T(1024)} %copy-done.32) | copy-start | bytes 24580
  966.6 33.1 %copy-start.37 = (f32[256]{0:T(256)S(1)}, f32[256]{0:T(256)}, u32[]{:S(2)}) copy-start(f32[256]{0:T(256)} %copy-done.36) | copy-start | bytes 3076
  999.8 17.1 copy-start.39
  999.8 17.1 copy-start.16
  999.8 17.1 copy-start.35
  1014.5 6.2 copy-start.41
  1016.8 3.9 copy-start.11
  1016.8 3.9 copy-start.17
  1016.8 3.9 copy-start.19
  1020.7 3.5 copy-start.13
  1024.2 491.8 %reduce-scatter.13.cloned.1.call-start = ((), (), s32[]{:S(2)}) async-start(), calls=%async_computation.23 | async-start | bytes 17301504 | tf_op jit(solution)/shard_map/reduce_scatter | solution.py:330
  1032.4 920.0 %reduce-scatter.11.cloned.1.call-start = ((), (), s32[]{:S(2)}) async-start(), calls=%async_computation.22 | async-start | bytes 51904512 | tf_op jit(solution)/shard_map/reduce_scatter | solution.py:328
  1148.6 804.3 %copy-start.47 = (f32[64]{0:T(128)}, f32[64]{0:T(128)S(1)}, u32[]{:S(2)}) copy-start(f32[64]{0:T(128)S(1)} %dynamic-slice.16) | copy-start | bytes 772
  (12 other events, 15.7 us)
Sparse Core Ops, SparseCore 0:
  62.5 80.5 all-gather.11
  144.9 52.9 all-gather.13
  199.5 80.7 all-gather.17
  282.0 52.9 all-gather.15
  337.7 77.3 all-gather.9
  417.9 172.8 all-gather.7
  593.0 99.6 reduce-scatter.8
  696.6 88.4 reduce-scatter.14
  788.6 71.2 reduce-scatter.16
  877.9 111.5 reduce-scatter.6
  1024.3 123.4 all-reduce.27
  1150.6 365.3 reduce-scatter.12
  1523.0 429.3 reduce-scatter.10
where the time goes:
time: 1970 us; the launch traced here: 1960 us
  waiting for transfers between devices  1480 us (75%)
  matrix products  222 us (11%)
  local copies, waits for them, and re-layouts  76 us (4%)
  blocking collectives  67.2 us (3%)
  other arithmetic  54.1 us (3%)
  starting transfers between devices  32.9 us (2%)
    reduce_scatter x1, waiting for transfers between devices, local(): lax.psum_scatter(in_delta, ('fsdp', 'seq'), scatter_dimension=0, tiled=True)  436 us
    reduce_scatter x1, waiting for transfers between devices, local(): lax.psum_scatter(out_delta, ('fsdp', 'seq'), scatter_dimension=0, tiled=T...  361 us
    all_gather x1, waiting for transfers between devices, local(): lax.all_gather(in_weight, ('fsdp', 'seq'), axis=0, tiled=True)  164 us
    dot_general x4, matrix products, times_transposed(): lax.dot_general(left_side, right_side, (((1,), (1,)), ((), ())), preferre...  71.4 us
    all_gather x1, waiting for transfers between devices, local(): lax.all_gather(second_in, 'seq', axis=1, tiled=True)  65.9 us
    unnamed x14, waiting for transfers between devices  65.9 us
    dot_general x4, matrix products, transposed_times(): lax.dot_general(left_side, right_side, (((0,), (0,)), ((), ())), preferre...  59.3 us
    unnamed x2, blocking collectives  57 us
  transfers between devices with their start and end apart: 21, of which 16 were waited for; matrix products, arithmetic and copies ran while one was open for 16% of the time, Pallas kernels for 0%

commit v1 on v0

v1 whole, which is shorter than its diff:
```python
import functools

import jax
import jax.numpy as jnp
from jax import lax
from jax.experimental import pallas as pl
from jax.experimental.pallas import tpu as pltpu
from jax.sharding import PartitionSpec as P

HEADS = 16
HEAD_DIM = 128
ROT = 32

EPSILON = 1e-05
MASKED_SCORE = -1e30
AXES = ("fsdp", "seq")
F32 = jnp.float32
BF16 = jnp.bfloat16


def dot(left, right, contract, out=F32):
    return lax.dot_general(
        left, right, ((contract[:1], contract[1:]), ((), ())), preferred_element_type=out
    )


def shift_seq(block, step):
    count = lax.axis_size("seq")
    return lax.ppermute(block, "seq", [(i, (i + step) % count) for i in range(count)])


def flip_fsdp(block, mask):
    count = lax.axis_size("fsdp")
    return lax.ppermute(block, "fsdp", [(i, i ^ mask) for i in range(count)])


def cross_first(block):
    return lax.ppermute(block, "fsdp", [(i, i ^ (2 if i & 1 else 4)) for i in range(8)])


def cross_second(block):
    return lax.ppermute(block, "fsdp", [(i, i ^ (4 if i & 1 else 2)) for i in range(8)])


def cross_masks(place):
    odd = (place & 1) == 1
    return jnp.where(odd, 2, 4), jnp.where(odd, 4, 2)


def put(buffer, block, index):
    return lax.dynamic_update_slice_in_dim(buffer, block[None], index, 0)


def pick(blocks, index):
    return lax.dynamic_index_in_dim(blocks, index, 0, keepdims=False)


def gather_fsdp(block):
    count = lax.axis_size("fsdp")
    if count != 8:
        return lax.all_gather(block, "fsdp", axis=0)
    place = lax.axis_index("fsdp")
    first, second = cross_masks(place)
    by_second = cross_second(block)
    by_first = cross_first(block)
    far = cross_first(by_second)
    full = jnp.zeros((8,) + block.shape, block.dtype)
    full = put(full, block, place)
    full = put(full, flip_fsdp(block, 1), place ^ 1)
    full = put(full, by_second, place ^ second)
    full = put(full, flip_fsdp(by_second, 1), place ^ 1 ^ first)
    full = put(full, by_first, place ^ first)
    full = put(full, flip_fsdp(by_first, 1), place ^ 1 ^ second)
    full = put(full, far, place ^ 6)
    full = put(full, flip_fsdp(far, 1), place ^ 7)
    return full


def scatter_fsdp(blocks):
    count = lax.axis_size("fsdp")
    if count != 8:
        return lax.psum_scatter(blocks, "fsdp", scatter_dimension=0, tiled=False).astype(F32)
    place = lax.axis_index("fsdp")
    first, second = cross_masks(place)

    def paired(mask):
        other = flip_fsdp(pick(blocks, place ^ 1 ^ mask).astype(BF16), 1)
        return other.astype(F32)

    from_pair = {mask: paired(mask) for mask in (6, 2, 4, 0)}
    odd = (place & 1) == 1
    pair_first = jnp.where(odd, from_pair[2], from_pair[4])
    pair_second = jnp.where(odd, from_pair[4], from_pair[2])
    far = pick(blocks, place ^ 6).astype(F32) + from_pair[6]
    got_far = cross_first(far.astype(BF16)).astype(F32)
    near_first = pick(blocks, place ^ first).astype(F32) + pair_first
    got_first = cross_first(near_first.astype(BF16)).astype(F32)
    near_second = pick(blocks, place ^ second).astype(F32) + pair_second + got_far
    got_second = cross_second(near_second.astype(BF16)).astype(F32)
    return pick(blocks, place).astype(F32) + from_pair[0] + got_first + got_second


def gather_seq(block):
    count = lax.axis_size("seq")
    place = lax.axis_index("seq")
    full = jnp.zeros((count,) + block.shape, block.dtype)
    full = put(full, block, place)
    moving = block
    for step in range(1, count):
        moving = shift_seq(moving, 1)
        full = put(full, moving, (place - step) % count)
    return full.reshape((count * block.shape[0],) + block.shape[1:])


def scatter_seq(blocks):
    count = lax.axis_size("seq")
    place = lax.axis_index("seq")
    moving = pick(blocks, (place - 1) % count).astype(BF16)
    for step in range(2, count + 1):
        moving = shift_seq(moving, 1).astype(F32) + pick(blocks, (place - step) % count).astype(F32)
        if step < count:
            moving = moving.astype(BF16)
    return moving


def exchange_seq(blocks):
    count = lax.axis_size("seq")
    place = lax.axis_index("seq")
    full = jnp.zeros(blocks.shape, blocks.dtype)
    full = put(full, pick(blocks, place), place)
    for step in range(1, count):
        got = shift_seq(pick(blocks, (place + step) % count), step)
        full = put(full, got, (place - step) % count)
    return full


def gather_small(vector):
    seq_count, fsdp_count = lax.axis_size("seq"), lax.axis_size("fsdp")
    seq_place, fsdp_place = lax.axis_index("seq"), lax.axis_index("fsdp")
    parts = jnp.stack([vector] + [shift_seq(vector, step) for step in range(1, seq_count)])
    parts = parts[(seq_place - jnp.arange(seq_count)) % seq_count]
    parts = jnp.stack([parts] + [flip_fsdp(parts, mask) for mask in range(1, fsdp_count)])
    return parts[fsdp_place ^ jnp.arange(fsdp_count)]


def scatter_small(everywhere, rows):
    seq_count, fsdp_count = lax.axis_size("seq"), lax.axis_size("fsdp")
    seq_place, fsdp_place = lax.axis_index("seq"), lax.axis_index("fsdp")
    by_seq = jnp.moveaxis(everywhere, 1, 0)
    total = pick(by_seq, seq_place)
    for step in range(1, seq_count):
        total = total + shift_seq(pick(by_seq, (seq_place + step) % seq_count), step)
    by_fsdp = jnp.concatenate([total, rows], axis=1)
    result = pick(by_fsdp, fsdp_place)
    for mask in range(1, fsdp_count):
        result = result + flip_fsdp(pick(by_fsdp, fsdp_place ^ mask), mask)
    return result


def rotary_tables(length):
    halves = jnp.arange(ROT // 2, dtype=F32)
    frequency = 1.0 / 10000.0 ** (halves * 2.0 / ROT)
    angles = jnp.arange(length, dtype=jnp.int32).astype(F32)[:, None] * frequency[None, :]
    cosine, sine = jnp.cos(angles), jnp.sin(angles)
    rest = jnp.zeros((length, HEAD_DIM - ROT), F32)
    nothing = jnp.zeros_like(sine)
    return (
        jnp.concatenate([cosine, cosine, rest + 1.0], axis=1),
        jnp.concatenate([-sine, nothing, rest], axis=1),
        jnp.concatenate([nothing, sine, rest], axis=1),
    )


def turn(values, cosine, lower, upper):
    half = ROT // 2
    return (
        values * cosine
        + pltpu.roll(values, HEAD_DIM - half, 1) * lower
        + pltpu.roll(values, half, 1) * upper
    )


def masked_probs(query, key_rows, first_row, used):
    scores = dot(query, key_rows, (1, 1)) * HEAD_DIM ** (-0.5)
    rows = first_row + lax.broadcasted_iota(jnp.int32, scores.shape, 0)
    columns = lax.broadcasted_iota(jnp.int32, scores.shape, 1)
    scores = jnp.where((columns <= rows) & (columns < used), scores, MASKED_SCORE)
    weights = jnp.exp(scores - jnp.max(scores, axis=1, keepdims=True))
    return weights / jnp.sum(weights, axis=1, keepdims=True)


def attend_kernel(rows, used_ref, q_in, k_in, v_in, cosine, lower, upper, q_out, k_out, v_out, mixed):
    length = q_in.shape[0]
    tables = (cosine[...], lower[...], upper[...])
    q_out[...] = turn(q_in[...], *tables).astype(BF16)
    k_out[...] = turn(k_in[...], *tables).astype(BF16)
    v_out[...] = v_in[...].astype(BF16)
    for start in range(0, length, rows):
        stop = start + rows
        probs = masked_probs(q_out[start:stop], k_out[:stop], start, used_ref[0])
        mixed[start:stop] = dot(probs.astype(BF16), v_out[:stop], (1, 0)).astype(BF16)


def attend_back_kernel(
    rows, used_ref, query, key_rows, value_rows, delta, cosine, lower, upper, q_out, k_out, v_out, k_sum, v_sum
):
    length = query.shape[0]
    scale = HEAD_DIM ** (-0.5)
    k_sum[...] = jnp.zeros_like(k_sum)
    v_sum[...] = jnp.zeros_like(v_sum)
    for start in range(0, length, rows):
        stop = start + rows
        block, block_delta = query[start:stop], delta[start:stop]
        probs = masked_probs(block, key_rows[:stop], start, used_ref[0])
        prob_delta = dot(block_delta, value_rows[:stop], (1, 1))
        row_dot = jnp.sum(probs * prob_delta, axis=1, keepdims=True)
        score_delta = (probs * (prob_delta - row_dot)).astype(BF16)
        query_delta = (dot(score_delta, key_rows[:stop], (1, 0)) * scale).astype(BF16).astype(F32)
        q_out[start:stop] = turn(
            query_delta, cosine[start:stop], -lower[start:stop], -upper[start:stop]
        ).astype(BF16)
        k_sum[:stop] += dot(score_delta, block, (0, 0))
        v_sum[:stop] += dot(probs.astype(BF16), block_delta, (0, 0))
    key_delta = (k_sum[...] * scale).astype(BF16).astype(F32)
    k_out[...] = turn(key_delta, cosine[...], -lower[...], -upper[...]).astype(BF16)
    v_out[...] = v_sum[...].astype(BF16)


def head_spec(length, shift):
    return pl.BlockSpec((length, HEAD_DIM), lambda head: (0, head + shift))


def attend(joined, tables, used, heads):
    length = joined.shape[0]
    table = pl.BlockSpec((length, HEAD_DIM), lambda head: (0, 0))
    shape = jax.ShapeDtypeStruct((length, heads * HEAD_DIM), BF16)
    return pl.pallas_call(
        functools.partial(attend_kernel, min(256, length)),
        grid=(heads,),
        in_specs=[pl.BlockSpec(memory_space=pltpu.SMEM)]
        + [head_spec(length, part * heads) for part in range(3)]
        + [table] * 3,
        out_specs=[head_spec(length, 0)] * 4,
        out_shape=[shape] * 4,
        name="attend",
    )(used, joined, joined, joined, *tables)


def attend_back(query, key_rows, value_rows, delta, tables, used, heads):
    length = query.shape[0]
    table = pl.BlockSpec((length, HEAD_DIM), lambda head: (0, 0))
    shape = jax.ShapeDtypeStruct((length, heads * HEAD_DIM), BF16)
    return pl.pallas_call(
        functools.partial(attend_back_kernel, min(256, length)),
        grid=(heads,),
        in_specs=[pl.BlockSpec(memory_space=pltpu.SMEM)] + [head_spec(length, 0)] * 4 + [table] * 3,
        out_specs=[head_spec(length, 0)] * 3,
        out_shape=[shape] * 3,
        scratch_shapes=[pltpu.VMEM((length, HEAD_DIM), F32)] * 2,
        name="attend_back",
    )(used, query, key_rows, value_rows, delta, *tables)


def normed(values):
    centred = values - jnp.mean(values, axis=-1, keepdims=True)
    scale = lax.rsqrt(jnp.mean(centred * centred, axis=-1, keepdims=True) + EPSILON)
    return centred * scale, scale


def gelu_pair(values):
    cumulative = 0.5 * (1.0 + lax.erf(values * 0.5**0.5))
    density = jnp.exp(-0.5 * values * values) * (0.5 / jnp.pi) ** 0.5
    return values * cumulative, cumulative + values * density


def after(value, *earlier):
    return lax.optimization_barrier((value,) + earlier)[0]


def local(
    hidden_in,
    lengths,
    cotangent,
    in_weight,
    in_bias,
    out_weight,
    out_bias,
    up_weight,
    up_bias,
    down_weight,
    down_bias,
    first_gain,
    first_shift,
    second_gain,
    second_shift,
):
    tokens, width = hidden_in.shape[1:]
    fsdp_count, seq_count = lax.axis_size("fsdp"), lax.axis_size("seq")
    fsdp_place, seq_place = lax.axis_index("fsdp"), lax.axis_index("seq")
    length = tokens * seq_count
    heads = HEADS // seq_count
    head_width = heads * HEAD_DIM
    hidden = up_weight.shape[0] * fsdp_count

    own = hidden_in.reshape(tokens, width)
    full = gather_seq(own)
    positions = seq_place * tokens + jnp.arange(tokens, dtype=jnp.int32)
    keep = (positions < lengths[0])[:, None]
    delta_own = jnp.where(keep, cotangent.reshape(tokens, width), jnp.zeros((), BF16))
    delta = gather_seq(after(delta_own, full))

    small = [in_bias, out_bias, down_bias, first_gain, first_shift, second_gain, second_shift]
    sizes = [member.shape[0] for member in small]
    everywhere = gather_small(jnp.concatenate(small + [up_bias]))
    at, whole = 0, []
    for size in sizes:
        whole.append(everywhere[:, :, at : at + size].reshape(-1).astype(F32))
        at += size
    in_offset, out_offset, down_offset, gain_one, shift_one, gain_two, shift_two = whole
    in_offset = lax.dynamic_index_in_dim(
        in_offset.reshape(3, seq_count, head_width), seq_place, 1, keepdims=False
    ).reshape(1, 3 * head_width)
    up_offset = lax.dynamic_index_in_dim(everywhere[:, :, at:], seq_place, 1, keepdims=False)
    up_offset = up_offset.reshape(1, hidden).astype(F32)

    rows = in_weight.shape[0]
    by_heads = in_weight.reshape(rows, 3, seq_count, head_width).transpose(2, 0, 1, 3)
    by_heads = exchange_seq(by_heads.reshape(seq_count, rows, 3 * head_width))
    by_heads = by_heads.reshape(seq_count * rows, 3 * head_width)
    up = gather_fsdp(up_weight).reshape(hidden, width)
    in_matrix = gather_fsdp(after(by_heads, up)).reshape(width, 3 * head_width)
    down = gather_fsdp(after(down_weight, in_matrix)).reshape(hidden, width)
    total = fsdp_count * seq_count
    mine = lax.ppermute(
        out_weight, AXES, [(i, (i % fsdp_count) * seq_count + i // fsdp_count) for i in range(total)]
    )
    out_matrix = gather_fsdp(after(mine, down)).reshape(head_width, width)

    unit, _ = normed(full.astype(F32))
    first_in = (unit * gain_one + shift_one).astype(BF16)
    second_in = (unit * gain_two + shift_two).astype(BF16)
    tables = rotary_tables(length)
    pre = dot(second_in, up, (1, 1)) + up_offset
    act, slope = gelu_pair(pre)
    act = act.astype(BF16)
    joined = dot(first_in, in_matrix, (1, 0)) + in_offset
    query, key_rows, value_rows, mixed = attend(joined, tables, lengths, heads)
    branches = dot(mixed, out_matrix, (1, 0)) + dot(act, down, (1, 0))
    summed = scatter_seq(branches.reshape(seq_count, tokens, width))
    source = own.astype(F32)
    layer_output = jnp.where(keep, source + summed + (out_offset + down_offset), 0.0)

    mixed_delta = dot(delta, out_matrix, (1, 1), BF16)
    pre_delta = (dot(delta, down, (1, 1)) * slope).astype(BF16)
    down_delta = dot(act, delta, (0, 0), BF16)
    down_gradient = scatter_fsdp(down_delta.reshape(fsdp_count, -1, width))
    out_delta = dot(mixed, delta, (0, 0), BF16)
    out_mine = scatter_fsdp(out_delta.reshape(fsdp_count, -1, width))
    query_delta, key_delta, value_delta = attend_back(
        query, key_rows, value_rows, mixed_delta, tables, lengths, heads
    )
    joined_delta = jnp.concatenate([query_delta, key_delta, value_delta], axis=1)
    up_delta = dot(pre_delta, second_in, (0, 0), BF16)
    up_gradient = scatter_fsdp(up_delta.reshape(fsdp_count, -1, width))
    second_delta = dot(pre_delta, up, (1, 0))
    first_delta = dot(joined_delta, in_matrix, (1, 1))
    in_delta = dot(first_in, joined_delta, (0, 0), BF16)
    in_rows = scatter_fsdp(in_delta.reshape(fsdp_count, -1, 3 * head_width))

    unit_delta = first_delta * gain_one + second_delta * gain_two
    unit_delta = scatter_seq(unit_delta.reshape(seq_count, tokens, width))
    own_unit, own_scale = normed(source)
    source_delta = own_scale * (
        unit_delta
        - jnp.mean(unit_delta, axis=-1, keepdims=True)
        - own_unit * jnp.mean(unit_delta * own_unit, axis=-1, keepdims=True)
    )
    input_gradient = delta_own.astype(F32) + source_delta

    out_gradient = lax.ppermute(
        out_mine, AXES, [((i % fsdp_count) * seq_count + i // fsdp_count, i) for i in range(total)]
    )
    in_gradient = exchange_seq(in_rows.astype(BF16).reshape(seq_count, rows, 3 * head_width))
    in_gradient = in_gradient.reshape(seq_count, rows, 3, head_width).transpose(1, 2, 0, 3)
    in_gradient = in_gradient.reshape(rows, -1).astype(F32)

    in_sum = jnp.sum(joined_delta.astype(F32), axis=0).reshape(3, 1, head_width)
    in_sum = lax.dynamic_update_slice_in_dim(
        jnp.zeros((3, seq_count, head_width), F32), in_sum, seq_place, 1
    )
    bias_sum = jnp.sum(delta_own.astype(F32), axis=0)
    sums = [
        in_sum,
        bias_sum,
        jnp.sum(first_delta * unit, axis=0),
        jnp.sum(first_delta, axis=0),
        jnp.sum(second_delta * unit, axis=0),
        jnp.sum(second_delta, axis=0),
    ]
    sums = jnp.concatenate([member.reshape(fsdp_count, seq_count, -1) for member in sums], axis=2)
    up_sum = jnp.sum(pre_delta.astype(F32), axis=0).reshape(fsdp_count, -1)
    small_sums = scatter_small(sums, up_sum)
    at, pieces = 0, []
    for size in (sizes[0],) + (sizes[1],) * 5 + (up_bias.shape[0],):
        pieces.append(small_sums[at : at + size])
        at += size
    in_bias_gradient, bias_gradient, gain_one_g, shift_one_g, gain_two_g, shift_two_g, up_bias_g = pieces
    return (
        layer_output[None],
        input_gradient[None],
        in_gradient,
        in_bias_gradient,
        out_gradient,
        bias_gradient,
        up_gradient,
        up_bias_g,
        down_gradient,
        bias_gradient,
        gain_one_g,
        shift_one_g,
        gain_two_g,
        shift_two_g,
    )


def solution(mesh):
    tokens, matrix, vector = P("fsdp", "seq", None), P(AXES, None), P(AXES)
    return jax.shard_map(
        local,
        mesh=mesh,
        in_specs=(tokens, P("fsdp"), tokens, matrix, vector, matrix, vector, matrix, vector, matrix)
        + (vector,) * 5,
        out_specs=(tokens, tokens, matrix, vector, matrix, vector, matrix, vector, matrix)
        + (vector,) * 5,
        check_vma=False,
    )
```

time: 1970 us -> 741 us (0.38)
  waiting for transfers between devices: 1480 us -> 303 us
  matrix products: 222 us -> 130 us
  blocking collectives: 67.2 us -> 0 us
  starting transfers between devices: 32.9 us -> 88.2 us
  local copies, waits for them, and re-layouts: 76 us -> 109 us
  Pallas kernels: 0 us -> 31.6 us
    reduce_scatter x6 -> x0, waiting for transfers between devices: 797 us -> none  [the longest x1 436 us: local(): lax.psum_scatter(in_delta, ('fsdp', 'seq'), scatter_dimension=0, tiled=True)]
    all_gather x6 -> x0, waiting for transfers between devices: 421 us -> none  [the longest x1 164 us: local(): lax.all_gather(in_weight, ('fsdp', 'seq'), axis=0, tiled=True)]
    ppermute x0 -> x96, waiting for transfers between devices: none -> 303 us  [the longest x24 196 us: shift_seq(): lax.ppermute(block, 'seq', [(i, (i + step) % count) for i in range(count)])]
    all_to_all x8 -> x0, waiting for transfers between devices: 198 us -> none  [the longest x1 53.1 us: local(): lax.all_to_all(turned[1].astype(jnp.bfloat16), 'seq', split_axis=2, conca...]
    dot_general x26 -> x12, matrix products: 222 us -> 130 us  [dot(): lax.dot_general(left, right, ((contract[:1], contract[1:]), ((), ())), pr...]
    ppermute x0 -> x96, starting transfers between devices: none -> 88.2 us  [the longest x46 39.7 us: flip_fsdp(): return lax.ppermute(block, 'fsdp', [(i, i ^ mask) for i in range(count)])]
    unnamed x14 -> x0, waiting for transfers between devices: 65.9 us -> none
    unnamed x2 -> x0, blocking collectives: 57 us -> none
  transfers between devices with their start and end apart: 21 -> 96, of which waited for: 16 -> 36; matrix products, arithmetic and copies ran while one was open for 16% -> 36% of each run, Pallas kernels for 0% -> 2%
where the time goes in v1:
time: 741 us; the launch traced here: 731 us
  waiting for transfers between devices  303 us (41%)
  matrix products  130 us (18%)
  local copies, waits for them, and re-layouts  109 us (15%)
  starting transfers between devices  88.2 us (12%)
  other arithmetic  65.3 us (9%)
  Pallas kernels  31.6 us (4%)
    ppermute x24, waiting for transfers between devices, shift_seq(): lax.ppermute(block, 'seq', [(i, (i + step) % count) for i in range(count)])  196 us
    dot_general x12, matrix products, dot(): lax.dot_general(left, right, ((contract[:1], contract[1:]), ((), ())), pr...  130 us
    ppermute x16, waiting for transfers between devices, cross_first(): lax.ppermute(block, 'fsdp', [(i, i ^ (2 if i & 1 else 4)) for i in range(...  68.5 us
    ppermute x46, starting transfers between devices, flip_fsdp(): return lax.ppermute(block, 'fsdp', [(i, i ^ mask) for i in range(count)])  39.7 us
    dynamic_update_slice x46, local copies, waits for them, and re-layouts, put(): return lax.dynamic_update_slice_in_dim(buffer, block[None], index, 0)  27.7 us
    ppermute x46, waiting for transfers between devices, flip_fsdp(): return lax.ppermute(block, 'fsdp', [(i, i ^ mask) for i in range(count)])  24.6 us
    dot_general x4, local copies, waits for them, and re-layouts, dot(): lax.dot_general(left, right, ((contract[:1], contract[1:]), ((), ())), pr...  21.7 us
    ppermute x24, starting transfers between devices, shift_seq(): lax.ppermute(block, 'seq', [(i, (i + step) % count) for i in range(count)])  17.6 us
  transfers between devices with their start and end apart: 96, of which 36 were waited for; matrix products, arithmetic and copies ran while one was open for 36% of the time, Pallas kernels for 2%

profile of v1, /device:TPU:0, one launch (start us, length us, event | category | flops | bytes accessed | tf_op | source)
XLA Modules:
  0.0 730.7 jit_solution(16087635324910963995)
XLA Ops:
  0.7 5.5 concatenate.21
  6.2 5.0 collective-permute-start.5
  45.3 2.8 collective-permute-done.8
  51.8 3.0 collective-permute-done.10
  56.4 3.0 collective-permute-done.11
  59.4 3.9 collective-permute-done.12
  66.1 24.8 %collective-permute-done.13 = bf16[64,1536]{1,0:T(8,128)(2,1)} collective-permute-done((bf16[64,1536]{1,0:T(8,128)(2,1)}, bf16[64,1536]{1,0:T(8,128)(2,1)}, u32[]{:S(2)}, u32[]{:S(2)}) %collective-permute-start.13) | collective-permute-done | bytes 196640 | tf_op jit(solution)/shard_map/ppermute | solution.py:29
  92.9 9.6 %collective-permute-done.14 = bf16[64,1536]{1,0:T(8,128)(2,1)S(1)} collective-permute-done((bf16[64,1536]{1,0:T(8,128)(2,1)}, bf16[64,1536]{1,0:T(8,128)(2,1)S(1)}, u32[]{:S(2)}, u32[]{:S(2)}) %collective-permute-start.14) | collective-permute-done | bytes 196640 | tf_op jit(solution)/shard_map/ppermute | solution.py:29
  104.2 5.0 collective-permute-done.15
  115.5 8.7 %collective-permute-done.19 = bf16[256,2048]{1,0:T(8,128)(2,1)S(1)} collective-permute-done((bf16[256,2048]{1,0:T(8,128)(2,1)}, bf16[256,2048]{1,0:T(8,128)(2,1)S(1)}, u32[]{:S(2)}, u32[]{:S(2)}) %collective-permute-start.19) | collective-permute-done | bytes 1048608 | tf_op jit(solution)/shard_map/ppermute | solution.py:38
  128.9 9.0 %collective-permute-done.1 = bf16[256,2048]{1,0:T(8,128)(2,1)S(1)} collective-permute-done((bf16[256,2048]{1,0:T(8,128)(2,1)}, bf16[256,2048]{1,0:T(8,128)(2,1)S(1)}, u32[]{:S(2)}, u32[]{:S(2)}) %collective-permute-start.1) | collective-permute-done | bytes 1048608 | tf_op jit(solution)/shard_map/ppermute | solution.py:29
  137.9 22.5 %collective-permute-done.49 = bf16[256,2048]{1,0:T(8,128)(2,1)S(1)} collective-permute-done((bf16[256,2048]{1,0:T(8,128)(2,1)S(1)}, bf16[256,2048]{1,0:T(8,128)(2,1)S(1)}, u32[]{:S(2)}, u32[]{:S(2)}) %collective-permute-start.49) | collective-permute-done | bytes 1048608 | tf_op jit(solution)/shard_map/ppermute | solution.py:29
  171.8 11.1 %collective-permute-done.2 = bf16[256,2048]{1,0:T(8,128)(2,1)S(1)} collective-permute-done((bf16[256,2048]{1,0:T(8,128)(2,1)S(1)}, bf16[256,2048]{1,0:T(8,128)(2,1)S(1)}, u32[]{:S(2)}, u32[]{:S(2)}) %collective-permute-start.2) | collective-permute-done | bytes 1048608 | tf_op jit(solution)/shard_map/ppermute | solution.py:29
  183.9 2.8 convert_reduce_fusion
  186.7 3.4 fusion.8
  191.8 13.0 %collective-permute-done.50 = bf16[256,2048]{1,0:T(8,128)(2,1)S(1)} collective-permute-done((bf16[256,2048]{1,0:T(8,128)(2,1)S(1)}, bf16[256,2048]{1,0:T(8,128)(2,1)S(1)}, u32[]{:S(2)}, u32[]{:S(2)}) %collective-permute-start.50) | collective-permute-done | bytes 1048608 | tf_op jit(solution)/shard_map/ppermute | solution.py:29
  205.9 5.7 fusion.5
  212.3 11.3 %collective-permute-done.28 = bf16[256,1536]{1,0:T(8,128)(2,1)S(1)} collective-permute-done((bf16[256,1536]{1,0:T(8,128)(2,1)S(1)}, bf16[256,1536]{1,0:T(8,128)(2,1)S(1)}, u32[]{:S(2)}, u32[]{:S(2)}) %collective-permute-start.28) | collective-permute-done | bytes 786464 | tf_op jit(solution)/shard_map/ppermute | solution.py:38
  226.0 8.6 %convolution_add_fusion.q_in.k_in.v_in = f32[1024,1536]{1,0:T(8,128)} fusion(bf16[1024,2048]{1,0:T(8,128)(2,1)S(1)} %bitcast.382, bf16[2048,1536]{1,0:T(8,128)(2,1)S(1)} %bitcast.370, f32[1536]{0:T(1024)S(1)} %add.558), kind=kOutput, calls=%fused_computation.42 | convolution fusion | flops 6444023808 | bytes 16783360 | tf_op jit(solution)/shard_map/dot_general | solution.py:22
  234.6 14.5 %attend.1 = (bf16[1024,512]{1,0:T(8,128)(2,1)}, bf16[1024,512]{1,0:T(8,128)(2,1)}, bf16[1024,512]{1,0:T(8,128)(2,1)}, bf16[1024,512]{1,0:T(8,128)(2,1)}) custom-call(s32[1]{0:T(128)} %copy.129.used_ref, f32[1024,1536]{1,0:T(8,128)} %convolution_add_fusion.q_in.k_in.v_in, f32[1024,1536]{1,0:T(8,128)} %convolution_add_fusion.q_in.k_in.v_in, ...), custom_call_target="tpu_custom_call" | custom-call | tf_op jit(solution)/shard_map/attend/pallas_call | solution.py:237
  251.4 4.9 fusion.115
  261.5 12.8 %fusion.112 = f32[1024,2048]{1,0:T(8,128)S(1)} fusion(bf16[1024,2048]{1,0:T(8,128)(2,1)} %bitcast.380, bf16[2048,2048]{1,0:T(8,128)(2,1)} %bitcast.363), kind=kOutput, calls=%fused_computation.297 | convolution fusion | flops 8589934592 | bytes 20971520 | tf_op jit(solution)/shard_map/dot_general | solution.py:22
  280.8 5.5 collective-permute-done.80
  290.2 7.1 collective-permute-done.77
  301.7 7.4 %collective-permute-start.35 = (bf16[256,2048]{1,0:T(8,128)(2,1)S(1)}, bf16[256,2048]{1,0:T(8,128)(2,1)S(1)}, u32[]{:S(2)}, u32[]{:S(2)}) collective-permute-start(bf16[256,2048]{1,0:T(8,128)(2,1)S(1)} %collective-permute-done.34), channel_id=1, source_target_pairs={{0,4},{4,0},{8,12},{12,8},{16,20},{20,16},{24,28},{28,24},{1,5},{5... | collective-permute-start | bytes 3145736 | tf_op jit(solution)/shard_map/ppermute | solution.py:34
  310.6 3.1 collective-permute-done.36
  313.7 14.8 %collective-permute-start.37 = (bf16[256,2048]{1,0:T(8,128)(2,1)S(1)}, bf16[256,2048]{1,0:T(8,128)(2,1)S(1)}, u32[]{:S(2)}, u32[]{:S(2)}) collective-permute-start(bf16[256,2048]{1,0:T(8,128)(2,1)S(1)} %collective-permute-done.36), channel_id=1, source_target_pairs={{0,4},{4,0},{8,12},{12,8},{16,20},{20,16},{24,28},{28,24},{1,5},{5... | collective-permute-start | bytes 3145736 | tf_op jit(solution)/shard_map/ppermute | solution.py:34
  333.8 11.6 %fusion.25 = f32[1024,2048]{1,0:T(8,128)} fusion(bf16[2048,2048]{1,0:T(8,128)(2,1)S(1)} %bitcast.367, f32[1024,2048]{1,0:T(8,128)S(1)} %fusion.112, f32[2048]{0:T(1024)S(1)} %bitcast.385), kind=kOutput, calls=%fused_computation.43 | convolution fusion | flops 8602517504 | bytes 25174016 | tf_op jit(solution)/shard_map/dot_general | solution.py:22
  345.5 17.8 %convert_reduce_fusion.1 = (f32[2048]{0:T(1024)S(1)}, bf16[1024,2048]{1,0:T(8,128)(2,1)}, f32[1024,2048]{1,0:T(8,128)}) fusion(f32[1024,2048]{1,0:T(8,128)S(1)} %fusion.112, f32[2048]{0:T(1024)S(1)} %bitcast.386, bf16[1024,2048]{1,0:T(8,128)(2,1)} %bitcast.377, bf16[2048,2048]{1,0:T(8,128)(2,1)} %bitcast.368), kind=kOutput, calls=%fused_computation.33 | convolution fusion | flops 8617195520 | bytes 33570816 | tf_op jit(solution)/shard_map/dot_general | solution.py:22
  363.3 11.7 %fusion.24 = (bf16[2048,1024]{0,1:T(8,128)(2,1)}, bf16[2048,1024]{0,1:T(8,128)(2,1)}) fusion(f32[1024,2048]{1,0:T(8,128)} %copy-done.6, f32[2048]{0:T(1024)S(1)} %bitcast.387, f32[1024,2048]{1,0:T(8,128)} %get-tuple-element.118), kind=kLoop, calls=%fused_computation.32 | loop fusion | flops 27262976 | bytes 25174016 | tf_op jit(solution)/shard_map/convert_element_type | solution.py:345
  375.1 6.4 copy.52
  381.5 12.1 %fusion.116 = bf16[8,256,2048]{2,1,0:T(8,128)(2,1)S(1)} fusion(bf16[8,256,1024]{2,1,0:T(8,128)(2,1)} %bitcast.373, bf16[1024,2048,1]{1,0,2:T(8,128)(2,1)} %bitcast.381), kind=kOutput, calls=%fused_computation.301 | convolution fusion | flops 8589934592 | bytes 16777216 | tf_op jit(solution)/shard_map/dot_general | solution.py:22
  393.6 2.5 dynamic-slice_bitcast_fusion.7
  398.2 6.4 copy.53
  404.6 11.9 %fusion.117 = bf16[8,256,2048]{2,1,0:T(8,128)(2,1)S(1)} fusion(bf16[8,256,1024]{2,1,0:T(8,128)(2,1)} %bitcast.375, bf16[1024,2048,1]{1,0,2:T(8,128)(2,1)} %bitcast.378), kind=kOutput, calls=%fused_computation.302 | convolution fusion | flops 8589934592 | bytes 16777216 | tf_op jit(solution)/shard_map/dot_general | solution.py:22
  418.7 3.4 copy-done.4
  424.7 4.3 collective-permute-done.43
  430.5 3.4 fusion.113.delta
  433.9 17.1 %attend_back.1 = (bf16[1024,512]{1,0:T(8,128)(2,1)}, bf16[1024,512]{1,0:T(8,128)(2,1)}, bf16[1024,512]{1,0:T(8,128)(2,1)}) custom-call(s32[1]{0:T(128)} %copy.129.used_ref, bf16[1024,512]{1,0:T(8,128)(2,1)} %get-tuple-element.29.query, bf16[1024,512]{1,0:T(8,128)(2,1)} %get-tuple-element.30.key_rows, bf16[1024,512]{1,0:T(8,128)(2,1)} %get-tuple-element.31.value_rows, ...), custom_call_target="tpu_custom_call" | custom-call | tf_op jit(solution)/shard_map/attend_back/pallas_call | solution.py:253
  454.3 12.0 %fusion.114 = f32[1024,2048]{1,0:T(8,128)} fusion(bf16[1024,1536]{1,0:T(8,128)(2,1)S(1)} %constant_dynamic-update-slice_fusion.9, bf16[2048,1536]{1,0:T(8,128)(2,1)} %bitcast.371), kind=kOutput, calls=%fused_computation.299 | convolution fusion | flops 6442450944 | bytes 17825792 | tf_op jit(solution)/shard_map/dot_general | solution.py:22
  467.5 5.6 convolution_add_fusion.1
  473.2 18.8 %fusion.108 = (f32[2048]{0:T(1024)S(1)}, f32[2048]{0:T(1024)S(1)}, f32[1024,2048]{1,0:T(8,128)}, f32[2048]{0:T(1024)S(1)}, f32[2048]{0:T(1024)S(1)}, /*index=5*/bf16[2048,1024]{0,1:T(8,128)(2,1)}) fusion(f32[1024]{0:T(1024)S(1)} %bitcast.391, f32[1024]{0:T(1024)S(1)} %bitcast.392, bf16[4,256,2048]{2,1,0:T(8,128)(2,1)} %bitcast_dynamic-update-slice_fusion.20, ...), kind=kOutput, calls=%fused_computation.294 | convolution fusion | flops 8621383680 | bytes 37814272 | tf_op jit(solution)/shard_map/dot_general | solution.py:22
  492.0 6.5 copy.51
  498.5 10.9 %fusion.28 = bf16[8,256,1536]{2,1,0:T(8,128)(2,1)} fusion(bf16[8,256,1024]{2,1,0:T(8,128)(2,1)} %bitcast.374, bf16[1024,1536]{1,0:T(8,128)(2,1)S(1)} %copy-done.13), kind=kOutput, calls=%fused_computation.47 | convolution fusion | flops 6442450944 | bytes 13631488 | tf_op jit(solution)/shard_map/dot_general | solution.py:22
  512.3 3.4 dynamic-slice_bitcast_fusion.11
  518.2 2.9 collective-permute-start.71
  536.8 19.4 %collective-permute-done.51 = bf16[256,2048]{1,0:T(8,128)(2,1)S(1)} collective-permute-done((bf16[256,2048]{1,0:T(8,128)(2,1)S(1)}, bf16[256,2048]{1,0:T(8,128)(2,1)S(1)}, u32[]{:S(2)}, u32[]{:S(2)}) %collective-permute-start.51) | collective-permute-done | bytes 1048608 | tf_op jit(solution)/shard_map/ppermute | solution.py:29
  558.2 20.1 %collective-permute-done.45 = bf16[256,2048]{1,0:T(8,128)(2,1)S(1)} collective-permute-done((bf16[256,2048]{1,0:T(8,128)(2,1)S(1)}, bf16[256,2048]{1,0:T(8,128)(2,1)S(1)}, u32[]{:S(2)}, u32[]{:S(2)}) %collective-permute-start.45) | collective-permute-done | bytes 1048608 | tf_op jit(solution)/shard_map/ppermute | solution.py:29
  581.2 2.6 fusion.40
  584.1 8.9 %collective-permute-done.94 = bf16[256,2048]{1,0:T(8,128)(2,1)S(1)} collective-permute-done((bf16[256,2048]{1,0:T(8,128)(2,1)S(1)}, bf16[256,2048]{1,0:T(8,128)(2,1)S(1)}, u32[]{:S(2)}, u32[]{:S(2)}) %collective-permute-start.94) | collective-permute-done | bytes 1048608 | tf_op jit(solution)/shard_map/ppermute | solution.py:38
  593.1 2.6 fusion.45
  597.1 8.6 %collective-permute-done.59 = bf16[256,1536]{1,0:T(8,128)(2,1)} collective-permute-done((bf16[256,1536]{1,0:T(8,128)(2,1)S(1)}, bf16[256,1536]{1,0:T(8,128)(2,1)}, u32[]{:S(2)}, u32[]{:S(2)}) %collective-permute-start.59) | collective-permute-done | bytes 786464 | tf_op jit(solution)/shard_map/ppermute | solution.py:38
  608.6 12.4 %collective-permute-done.52 = bf16[256,2048]{1,0:T(8,128)(2,1)S(1)} collective-permute-done((bf16[256,2048]{1,0:T(8,128)(2,1)S(1)}, bf16[256,2048]{1,0:T(8,128)(2,1)S(1)}, u32[]{:S(2)}, u32[]{:S(2)}) %collective-permute-start.52) | collective-permute-done | bytes 1048608 | tf_op jit(solution)/shard_map/ppermute | solution.py:29
  623.2 18.1 %collective-permute-done.46 = bf16[256,2048]{1,0:T(8,128)(2,1)S(1)} collective-permute-done((bf16[256,2048]{1,0:T(8,128)(2,1)S(1)}, bf16[256,2048]{1,0:T(8,128)(2,1)S(1)}, u32[]{:S(2)}, u32[]{:S(2)}) %collective-permute-start.46) | collective-permute-done | bytes 1048608 | tf_op jit(solution)/shard_map/ppermute | solution.py:29
  645.5 3.2 fusion.57
  648.7 10.8 %collective-permute-done.57 = bf16[256,1536]{1,0:T(8,128)(2,1)S(1)} collective-permute-done((bf16[256,1536]{1,0:T(8,128)(2,1)S(1)}, bf16[256,1536]{1,0:T(8,128)(2,1)S(1)}, u32[]{:S(2)}, u32[]{:S(2)}) %collective-permute-start.57) | collective-permute-done | bytes 786464 | tf_op jit(solution)/shard_map/ppermute | solution.py:38
  661.6 8.5 %collective-permute-done.95 = bf16[256,2048]{1,0:T(8,128)(2,1)S(1)} collective-permute-done((bf16[256,2048]{1,0:T(8,128)(2,1)S(1)}, bf16[256,2048]{1,0:T(8,128)(2,1)S(1)}, u32[]{:S(2)}, u32[]{:S(2)}) %collective-permute-start.95) | collective-permute-done | bytes 1048608 | tf_op jit(solution)/shard_map/ppermute | solution.py:42
  670.0 5.7 collective-permute-done.92
  675.7 3.2 fusion.54
  680.0 23.6 %collective-permute-done.61 = bf16[64,1536]{1,0:T(8,128)(2,1)S(1)} collective-permute-done((bf16[64,1536]{1,0:T(8,128)(2,1)S(1)}, bf16[64,1536]{1,0:T(8,128)(2,1)S(1)}, u32[]{:S(2)}, u32[]{:S(2)}) %collective-permute-start.61) | collective-permute-done | bytes 196640 | tf_op jit(solution)/shard_map/ppermute | solution.py:29
  704.3 6.6 collective-permute-done.62
  712.3 2.8 reshape.457
  717.3 3.3 reshape.444
  723.2 6.0 fusion.38
  (418 shorter events, 163.6 us)
Async XLA Ops:
  6.2 30.8 %collective-permute-start.5 = (bf16[832]{0:T(1024)(128)(2,1)S(1)}, bf16[832]{0:T(1024)(128)(2,1)S(1)}, u32[]{:S(2)}, u32[]{:S(2)}) collective-permute-start(bf16[832]{0:T(1024)(128)(2,1)S(1)} %concatenate.21), channel_id=1, source_target_pairs={{0,3},{1,0},{2,1},{3,2},{4,7},{5,4},{6,5},{7,6},{8,11},{9,8},{10,9... | collective-permute-start | bytes 5000 | tf_op jit(solution)/shard_map/ppermute | solution.py:29
  11.2 28.3 %collective-permute-start.4 = (bf16[832]{0:T(1024)(128)(2,1)S(1)}, bf16[832]{0:T(1024)(128)(2,1)S(1)}, u32[]{:S(2)}, u32[]{:S(2)}) collective-permute-start(bf16[832]{0:T(1024)(128)(2,1)S(1)} %concatenate.21), channel_id=1, source_target_pairs={{0,2},{1,3},{2,0},{3,1},{4,6},{5,7},{6,4},{7,5},{8,10},{9,11},{10,... | collective-permute-start | bytes 5000 | tf_op jit(solution)/shard_map/ppermute | solution.py:29
  11.2 28.4 %collective-permute-start.3 = (bf16[832]{0:T(1024)(128)(2,1)S(1)}, bf16[832]{0:T(1024)(128)(2,1)S(1)}, u32[]{:S(2)}, u32[]{:S(2)}) collective-permute-start(bf16[832]{0:T(1024)(128)(2,1)S(1)} %concatenate.21), channel_id=1, source_target_pairs={{0,1},{1,2},{2,3},{3,0},{4,5},{5,6},{6,7},{7,4},{8,9},{9,10},{10,1... | collective-permute-start | bytes 5000 | tf_op jit(solution)/shard_map/ppermute | solution.py:29
  12.2 103.3 %collective-permute-start.16 = (bf16[256,2048]{1,0:T(8,128)(2,1)}, bf16[256,2048]{1,0:T(8,128)(2,1)}, u32[]{:S(2)}, u32[]{:S(2)}) collective-permute-start(bf16[256,2048]{1,0:T(8,128)(2,1)} %param.22), channel_id=1, source_target_pairs={{0,4},{4,0},{8,12},{12,8},{16,20},{20,16},{24,28},{28,24},{1,5},{5... | collective-permute-start | bytes 3145736 | tf_op jit(solution)/shard_map/ppermute | solution.py:34
  12.2 97.7 %collective-permute-start.17 = (bf16[256,2048]{1,0:T(8,128)(2,1)}, bf16[256,2048]{1,0:T(8,128)(2,1)}, u32[]{:S(2)}, u32[]{:S(2)}) collective-permute-start(bf16[256,2048]{1,0:T(8,128)(2,1)} %param.22), channel_id=1, source_target_pairs={{0,8},{4,20},{8,0},{12,28},{16,24},{20,4},{24,16},{28,12},{1,9},{5... | collective-permute-start | bytes 3145736 | tf_op jit(solution)/shard_map/ppermute | solution.py:42
  37.0 75.0 %collective-permute-start.48 = (bf16[256,2048]{1,0:T(8,128)(2,1)S(1)}, bf16[256,2048]{1,0:T(8,128)(2,1)S(1)}, u32[]{:S(2)}, u32[]{:S(2)}) collective-permute-start(bf16[256,2048]{1,0:T(8,128)(2,1)S(1)} %get-tuple-element.32), channel_id=1, source_target_pairs={{0,1},{1,2},{2,3},{3,0},{4,5},{5,6},{6,7},{7,4},{8,9},{9,10},{10,1... | collective-permute-start | bytes 3145736 | tf_op jit(solution)/shard_map/ppermute | solution.py:29
  39.5 70.4 %collective-permute-start = (bf16[256,2048]{1,0:T(8,128)(2,1)S(1)}, bf16[256,2048]{1,0:T(8,128)(2,1)}, u32[]{:S(2)}, u32[]{:S(2)}) collective-permute-start(bf16[256,2048]{1,0:T(8,128)(2,1)S(1)} %bitcast.350), channel_id=1, source_target_pairs={{0,1},{1,2},{2,3},{3,0},{4,5},{5,6},{6,7},{7,4},{8,9},{9,10},{10,1... | collective-permute-start | bytes 3145736 | tf_op jit(solution)/shard_map/ppermute | solution.py:29
  63.4 27.6 %collective-permute-start.13 = (bf16[64,1536]{1,0:T(8,128)(2,1)}, bf16[64,1536]{1,0:T(8,128)(2,1)}, u32[]{:S(2)}, u32[]{:S(2)}) collective-permute-start(bf16[64,1536]{1,0:T(8,128)(2,1)} %get-tuple-element.94), channel_id=1, source_target_pairs={{0,1},{1,2},{2,3},{3,0},{4,5},{5,6},{6,7},{7,4},{8,9},{9,10},{10,1... | collective-permute-start | bytes 589832 | tf_op jit(solution)/shard_map/ppermute | solution.py:29
  109.2 15.0 %collective-permute-start.19 = (bf16[256,2048]{1,0:T(8,128)(2,1)}, bf16[256,2048]{1,0:T(8,128)(2,1)S(1)}, u32[]{:S(2)}, u32[]{:S(2)}) collective-permute-start(bf16[256,2048]{1,0:T(8,128)(2,1)} %param.22), channel_id=1, source_target_pairs={{0,16},{4,12},{8,24},{12,4},{16,0},{20,28},{24,8},{28,20},{1,17},{... | collective-permute-start | bytes 3145736 | tf_op jit(solution)/shard_map/ppermute | solution.py:38
  109.9 28.0 %collective-permute-start.1 = (bf16[256,2048]{1,0:T(8,128)(2,1)}, bf16[256,2048]{1,0:T(8,128)(2,1)S(1)}, u32[]{:S(2)}, u32[]{:S(2)}) collective-permute-start(bf16[256,2048]{1,0:T(8,128)(2,1)} %collective-permute-done), channel_id=1, source_target_pairs={{0,1},{1,2},{2,3},{3,0},{4,5},{5,6},{6,7},{7,4},{8,9},{9,10},{10,1... | collective-permute-start | bytes 3145736 | tf_op jit(solution)/shard_map/ppermute | solution.py:29
  109.9 28.0 %collective-permute-start.21 = (bf16[256,2048]{1,0:T(8,128)(2,1)}, bf16[256,2048]{1,0:T(8,128)(2,1)S(1)}, u32[]{:S(2)}, u32[]{:S(2)}) collective-permute-start(bf16[256,2048]{1,0:T(8,128)(2,1)} %collective-permute-done.17), channel_id=1, source_target_pairs={{0,16},{4,12},{8,24},{12,4},{16,0},{20,28},{24,8},{28,20},{1,17},{... | collective-permute-start | bytes 3145736 | tf_op jit(solution)/shard_map/ppermute | solution.py:38
  112.0 48.3 %collective-permute-start.49 = (bf16[256,2048]{1,0:T(8,128)(2,1)S(1)}, bf16[256,2048]{1,0:T(8,128)(2,1)S(1)}, u32[]{:S(2)}, u32[]{:S(2)}) collective-permute-start(bf16[256,2048]{1,0:T(8,128)(2,1)S(1)} %collective-permute-done.48), channel_id=1, source_target_pairs={{0,1},{1,2},{2,3},{3,0},{4,5},{5,6},{6,7},{7,4},{8,9},{9,10},{10,1... | collective-permute-start | bytes 3145736 | tf_op jit(solution)/shard_map/ppermute | solution.py:29
  115.5 47.1 %collective-permute-start.18 = (bf16[256,2048]{1,0:T(8,128)(2,1)}, bf16[256,2048]{1,0:T(8,128)(2,1)S(1)}, u32[]{:S(2)}, u32[]{:S(2)}) collective-permute-start(bf16[256,2048]{1,0:T(8,128)(2,1)} %collective-permute-done.17), channel_id=1, source_target_pairs={{0,4},{4,0},{8,12},{12,8},{16,20},{20,16},{24,28},{28,24},{1,5},{5... | collective-permute-start | bytes 3145736 | tf_op jit(solution)/shard_map/ppermute | solution.py:34
  124.2 40.5 %collective-permute-start.20 = (bf16[256,2048]{1,0:T(8,128)(2,1)S(1)}, bf16[256,2048]{1,0:T(8,128)(2,1)S(1)}, u32[]{:S(2)}, u32[]{:S(2)}) collective-permute-start(bf16[256,2048]{1,0:T(8,128)(2,1)S(1)} %collective-permute-done.19), channel_id=1, source_target_pairs={{0,4},{4,0},{8,12},{12,8},{16,20},{20,16},{24,28},{28,24},{1,5},{5... | collective-permute-start | bytes 3145736 | tf_op jit(solution)/shard_map/ppermute | solution.py:34
  137.9 44.9 %collective-permute-start.2 = (bf16[256,2048]{1,0:T(8,128)(2,1)S(1)}, bf16[256,2048]{1,0:T(8,128)(2,1)S(1)}, u32[]{:S(2)}, u32[]{:S(2)}) collective-permute-start(bf16[256,2048]{1,0:T(8,128)(2,1)S(1)} %collective-permute-done.1), channel_id=1, source_target_pairs={{0,1},{1,2},{2,3},{3,0},{4,5},{5,6},{6,7},{7,4},{8,9},{9,10},{10,1... | collective-permute-start | bytes 3145736 | tf_op jit(solution)/shard_map/ppermute | solution.py:29
  137.9 29.0 %collective-permute-start.22 = (bf16[256,2048]{1,0:T(8,128)(2,1)S(1)}, bf16[256,2048]{1,0:T(8,128)(2,1)S(1)}, u32[]{:S(2)}, u32[]{:S(2)}) collective-permute-start(bf16[256,2048]{1,0:T(8,128)(2,1)S(1)} %collective-permute-done.21), channel_id=1, source_target_pairs={{0,4},{4,0},{8,12},{12,8},{16,20},{20,16},{24,28},{28,24},{1,5},{5... | collective-permute-start | bytes 3145736 | tf_op jit(solution)/shard_map/ppermute | solution.py:34
  160.4 44.5 %collective-permute-start.50 = (bf16[256,2048]{1,0:T(8,128)(2,1)S(1)}, bf16[256,2048]{1,0:T(8,128)(2,1)S(1)}, u32[]{:S(2)}, u32[]{:S(2)}) collective-permute-start(bf16[256,2048]{1,0:T(8,128)(2,1)S(1)} %collective-permute-done.49), channel_id=1, source_target_pairs={{0,1},{1,2},{2,3},{3,0},{4,5},{5,6},{6,7},{7,4},{8,9},{9,10},{10,1... | collective-permute-start | bytes 3145736 | tf_op jit(solution)/shard_map/ppermute | solution.py:29
  167.9 44.3 %collective-permute-start.23 = (bf16[256,1536]{1,0:T(8,128)(2,1)}, bf16[256,1536]{1,0:T(8,128)(2,1)S(1)}, u32[]{:S(2)}, u32[]{:S(2)}) collective-permute-start(bf16[256,1536]{1,0:T(8,128)(2,1)} %bitcast.23), channel_id=1, source_target_pairs={{0,4},{4,0},{8,12},{12,8},{16,20},{20,16},{24,28},{28,24},{1,5},{5... | collective-permute-start | bytes 2359304 | tf_op jit(solution)/shard_map/ppermute | solution.py:34
  167.9 43.7 %collective-permute-start.24 = (bf16[256,1536]{1,0:T(8,128)(2,1)}, bf16[256,1536]{1,0:T(8,128)(2,1)S(1)}, u32[]{:S(2)}, u32[]{:S(2)}) collective-permute-start(bf16[256,1536]{1,0:T(8,128)(2,1)} %bitcast.23), channel_id=1, source_target_pairs={{0,8},{4,20},{8,0},{12,28},{16,24},{20,4},{24,16},{28,12},{1,9},{5... | collective-permute-start | bytes 2359304 | tf_op jit(solution)/shard_map/ppermute | solution.py:42
  170.0 41.9 %collective-permute-start.26 = (bf16[256,1536]{1,0:T(8,128)(2,1)}, bf16[256,1536]{1,0:T(8,128)(2,1)S(1)}, u32[]{:S(2)}, u32[]{:S(2)}) collective-permute-start(bf16[256,1536]{1,0:T(8,128)(2,1)} %bitcast.23), channel_id=1, source_target_pairs={{0,16},{4,12},{8,24},{12,4},{16,0},{20,28},{24,8},{28,20},{1,17},{... | collective-permute-start | bytes 2359304 | tf_op jit(solution)/shard_map/ppermute | solution.py:38
  211.6 12.1 %collective-permute-start.25 = (bf16[256,1536]{1,0:T(8,128)(2,1)S(1)}, bf16[256,1536]{1,0:T(8,128)(2,1)S(1)}, u32[]{:S(2)}, u32[]{:S(2)}) collective-permute-start(bf16[256,1536]{1,0:T(8,128)(2,1)S(1)} %collective-permute-done.24), channel_id=1, source_target_pairs={{0,4},{4,0},{8,12},{12,8},{16,20},{20,16},{24,28},{28,24},{1,5},{5... | collective-permute-start | bytes 2359304 | tf_op jit(solution)/shard_map/ppermute | solution.py:34
  258.2 29.7 %collective-permute-start.32 = (bf16[256,2048]{1,0:T(8,128)(2,1)S(1)}, bf16[256,2048]{1,0:T(8,128)(2,1)S(1)}, u32[]{:S(2)}, u32[]{:S(2)}) collective-permute-start(bf16[256,2048]{1,0:T(8,128)(2,1)S(1)} %copy-done.20), channel_id=1, source_target_pairs={{0,8},{4,20},{8,0},{12,28},{16,24},{20,4},{24,16},{28,12},{1,9},{5... | collective-permute-start | bytes 3145736 | tf_op jit(solution)/shard_map/ppermute | solution.py:42
  258.6 15.8 %collective-permute-start.76 = (bf16[64,2048]{1,0:T(8,128)(2,1)}, bf16[64,2048]{1,0:T(8,128)(2,1)S(1)}, u32[]{:S(2)}, u32[]{:S(2)}) collective-permute-start(bf16[64,2048]{1,0:T(8,128)(2,1)} %get-tuple-element.84), channel_id=1, source_target_pairs={{0,4},{4,0},{8,12},{12,8},{16,20},{20,16},{24,28},{28,24},{1,5},{5... | collective-permute-start | bytes 786440 | tf_op jit(solution)/shard_map/ppermute | solution.py:34
  258.7 16.5 %collective-permute-start.75 = (bf16[64,2048]{1,0:T(8,128)(2,1)}, bf16[64,2048]{1,0:T(8,128)(2,1)S(1)}, u32[]{:S(2)}, u32[]{:S(2)}) collective-permute-start(bf16[64,2048]{1,0:T(8,128)(2,1)} %get-tuple-element.85), channel_id=1, source_target_pairs={{0,4},{4,0},{8,12},{12,8},{16,20},{20,16},{24,28},{28,24},{1,5},{5... | collective-permute-start | bytes 786440 | tf_op jit(solution)/shard_map/ppermute | solution.py:34
  260.2 15.1 %collective-permute-start.79 = (bf16[64,2048]{1,0:T(8,128)(2,1)S(1)}, bf16[64,2048]{1,0:T(8,128)(2,1)S(1)}, u32[]{:S(2)}, u32[]{:S(2)}) collective-permute-start(bf16[64,2048]{1,0:T(8,128)(2,1)S(1)} %fusion.79), channel_id=1, source_target_pairs={{0,16},{4,12},{8,24},{12,4},{16,0},{20,28},{24,8},{28,20},{1,17},{... | collective-permute-start | bytes 786440 | tf_op jit(solution)/shard_map/ppermute | solution.py:38
  274.3 26.7 %collective-permute-start.31 = (bf16[256,2048]{1,0:T(8,128)(2,1)S(1)}, bf16[256,2048]{1,0:T(8,128)(2,1)}, u32[]{:S(2)}, u32[]{:S(2)}) collective-permute-start(bf16[256,2048]{1,0:T(8,128)(2,1)S(1)} %copy-done.20), channel_id=1, source_target_pairs={{0,4},{4,0},{8,12},{12,8},{16,20},{20,16},{24,28},{28,24},{1,5},{5... | collective-permute-start | bytes 3145736 | tf_op jit(solution)/shard_map/ppermute | solution.py:34
  274.5 27.2 %collective-permute-start.34 = (bf16[256,2048]{1,0:T(8,128)(2,1)S(1)}, bf16[256,2048]{1,0:T(8,128)(2,1)S(1)}, u32[]{:S(2)}, u32[]{:S(2)}) collective-permute-start(bf16[256,2048]{1,0:T(8,128)(2,1)S(1)} %copy-done.20), channel_id=1, source_target_pairs={{0,16},{4,12},{8,24},{12,4},{16,0},{20,28},{24,8},{28,20},{1,17},{... | collective-permute-start | bytes 3145736 | tf_op jit(solution)/shard_map/ppermute | solution.py:38
  279.1 18.2 %collective-permute-start.77 = (bf16[64,2048]{1,0:T(8,128)(2,1)}, bf16[64,2048]{1,0:T(8,128)(2,1)}, u32[]{:S(2)}, u32[]{:S(2)}) collective-permute-start(bf16[64,2048]{1,0:T(8,128)(2,1)} %get-tuple-element.80), channel_id=1, source_target_pairs={{0,16},{4,12},{8,24},{12,4},{16,0},{20,28},{24,8},{28,20},{1,17},{... | collective-permute-start | bytes 786440 | tf_op jit(solution)/shard_map/ppermute | solution.py:38
  286.3 44.6 %collective-permute-start.30 = (bf16[64,2048]{1,0:T(8,128)(2,1)}, bf16[64,2048]{1,0:T(8,128)(2,1)S(1)}, u32[]{:S(2)}, u32[]{:S(2)}) collective-permute-start(bf16[64,2048]{1,0:T(8,128)(2,1)} %param.20), channel_id=1, source_target_pairs={{0,0},{1,4},{2,8},{3,12},{4,16},{5,20},{6,24},{7,28},{8,1},{9,5},{... | collective-permute-start | bytes 786440 | tf_op jit(solution)/shard_map/ppermute | solution.py:334
  287.9 40.6 %collective-permute-start.33 = (bf16[256,2048]{1,0:T(8,128)(2,1)S(1)}, bf16[256,2048]{1,0:T(8,128)(2,1)S(1)}, u32[]{:S(2)}, u32[]{:S(2)}) collective-permute-start(bf16[256,2048]{1,0:T(8,128)(2,1)S(1)} %collective-permute-done.32), channel_id=1, source_target_pairs={{0,4},{4,0},{8,12},{12,8},{16,20},{20,16},{24,28},{28,24},{1,5},{5... | collective-permute-start | bytes 3145736 | tf_op jit(solution)/shard_map/ppermute | solution.py:34
  297.3 16.4 %collective-permute-start.36 = (bf16[256,2048]{1,0:T(8,128)(2,1)S(1)}, bf16[256,2048]{1,0:T(8,128)(2,1)S(1)}, u32[]{:S(2)}, u32[]{:S(2)}) collective-permute-start(bf16[256,2048]{1,0:T(8,128)(2,1)S(1)} %collective-permute-done.32), channel_id=1, source_target_pairs={{0,16},{4,12},{8,24},{12,4},{16,0},{20,28},{24,8},{28,20},{1,17},{... | collective-permute-start | bytes 3145736 | tf_op jit(solution)/shard_map/ppermute | solution.py:38
  301.7 27.0 %collective-permute-start.35 = (bf16[256,2048]{1,0:T(8,128)(2,1)S(1)}, bf16[256,2048]{1,0:T(8,128)(2,1)S(1)}, u32[]{:S(2)}, u32[]{:S(2)}) collective-permute-start(bf16[256,2048]{1,0:T(8,128)(2,1)S(1)} %collective-permute-done.34), channel_id=1, source_target_pairs={{0,4},{4,0},{8,12},{12,8},{16,20},{20,16},{24,28},{28,24},{1,5},{5... | collective-permute-start | bytes 3145736 | tf_op jit(solution)/shard_map/ppermute | solution.py:34
  313.7 17.1 %collective-permute-start.37 = (bf16[256,2048]{1,0:T(8,128)(2,1)S(1)}, bf16[256,2048]{1,0:T(8,128)(2,1)S(1)}, u32[]{:S(2)}, u32[]{:S(2)}) collective-permute-start(bf16[256,2048]{1,0:T(8,128)(2,1)S(1)} %collective-permute-done.36), channel_id=1, source_target_pairs={{0,4},{4,0},{8,12},{12,8},{16,20},{20,16},{24,28},{28,24},{1,5},{5... | collective-permute-start | bytes 3145736 | tf_op jit(solution)/shard_map/ppermute | solution.py:34
  330.9 93.7 %collective-permute-start.38 = (bf16[64,2048]{1,0:T(8,128)(2,1)S(1)}, bf16[64,2048]{1,0:T(8,128)(2,1)S(1)}, u32[]{:S(2)}, u32[]{:S(2)}) collective-permute-start(bf16[64,2048]{1,0:T(8,128)(2,1)S(1)} %collective-permute-done.30), channel_id=1, source_target_pairs={{0,4},{4,0},{8,12},{12,8},{16,20},{20,16},{24,28},{28,24},{1,5},{5... | collective-permute-start | bytes 786440 | tf_op jit(solution)/shard_map/ppermute | solution.py:34
  331.4 90.7 %collective-permute-start.39 = (bf16[64,2048]{1,0:T(8,128)(2,1)S(1)}, bf16[64,2048]{1,0:T(8,128)(2,1)S(1)}, u32[]{:S(2)}, u32[]{:S(2)}) collective-permute-start(bf16[64,2048]{1,0:T(8,128)(2,1)S(1)} %collective-permute-done.30), channel_id=1, source_target_pairs={{0,8},{4,20},{8,0},{12,28},{16,24},{20,4},{24,16},{28,12},{1,9},{5... | collective-permute-start | bytes 786440 | tf_op jit(solution)/shard_map/ppermute | solution.py:42
  333.6 91.1 %collective-permute-start.41 = (bf16[64,2048]{1,0:T(8,128)(2,1)S(1)}, bf16[64,2048]{1,0:T(8,128)(2,1)S(1)}, u32[]{:S(2)}, u32[]{:S(2)}) collective-permute-start(bf16[64,2048]{1,0:T(8,128)(2,1)S(1)} %collective-permute-done.30), channel_id=1, source_target_pairs={{0,16},{4,12},{8,24},{12,4},{16,0},{20,28},{24,8},{28,20},{1,17},{... | collective-permute-start | bytes 786440 | tf_op jit(solution)/shard_map/ppermute | solution.py:38
  398.2 133.3 %collective-permute-start.86 = (bf16[256,2048]{1,0:T(8,128)(2,1)}, bf16[256,2048]{1,0:T(8,128)(2,1)}, u32[]{:S(2)}, u32[]{:S(2)}) collective-permute-start(bf16[256,2048]{1,0:T(8,128)(2,1)} %get-tuple-element.65), channel_id=1, source_target_pairs={{0,4},{4,0},{8,12},{12,8},{16,20},{20,16},{24,28},{28,24},{1,5},{5... | collective-permute-start | bytes 3145736 | tf_op jit(solution)/shard_map/ppermute | solution.py:34
  527.2 30.9 %collective-permute-start.84 = (bf16[256,2048]{1,0:T(8,128)(2,1)}, bf16[256,2048]{1,0:T(8,128)(2,1)S(1)}, u32[]{:S(2)}, u32[]{:S(2)}) collective-permute-start(bf16[256,2048]{1,0:T(8,128)(2,1)} %get-tuple-element.66), channel_id=1, source_target_pairs={{0,4},{4,0},{8,12},{12,8},{16,20},{20,16},{24,28},{28,24},{1,5},{5... | collective-permute-start | bytes 3145736 | tf_op jit(solution)/shard_map/ppermute | solution.py:34
  528.4 51.5 %collective-permute-start.83 = (bf16[256,2048]{1,0:T(8,128)(2,1)}, bf16[256,2048]{1,0:T(8,128)(2,1)S(1)}, u32[]{:S(2)}, u32[]{:S(2)}) collective-permute-start(bf16[256,2048]{1,0:T(8,128)(2,1)} %get-tuple-element.67), channel_id=1, source_target_pairs={{0,4},{4,0},{8,12},{12,8},{16,20},{20,16},{24,28},{28,24},{1,5},{5... | collective-permute-start | bytes 3145736 | tf_op jit(solution)/shard_map/ppermute | solution.py:34
  528.4 27.8 %collective-permute-start.51 = (bf16[256,2048]{1,0:T(8,128)(2,1)S(1)}, bf16[256,2048]{1,0:T(8,128)(2,1)S(1)}, u32[]{:S(2)}, u32[]{:S(2)}) collective-permute-start(bf16[256,2048]{1,0:T(8,128)(2,1)S(1)} %fusion.72), channel_id=1, source_target_pairs={{0,1},{1,2},{2,3},{3,0},{4,5},{5,6},{6,7},{7,4},{8,9},{9,10},{10,1... | collective-permute-start | bytes 3145736 | tf_op jit(solution)/shard_map/ppermute | solution.py:29
  533.7 44.5 %collective-permute-start.45 = (bf16[256,2048]{1,0:T(8,128)(2,1)S(1)}, bf16[256,2048]{1,0:T(8,128)(2,1)S(1)}, u32[]{:S(2)}, u32[]{:S(2)}) collective-permute-start(bf16[256,2048]{1,0:T(8,128)(2,1)S(1)} %fusion.71), channel_id=1, source_target_pairs={{0,1},{1,2},{2,3},{3,0},{4,5},{5,6},{6,7},{7,4},{8,9},{9,10},{10,1... | collective-permute-start | bytes 3145736 | tf_op jit(solution)/shard_map/ppermute | solution.py:29
  536.6 43.4 %collective-permute-start.91 = (bf16[256,2048]{1,0:T(8,128)(2,1)S(1)}, bf16[256,2048]{1,0:T(8,128)(2,1)S(1)}, u32[]{:S(2)}, u32[]{:S(2)}) collective-permute-start(bf16[256,2048]{1,0:T(8,128)(2,1)S(1)} %copy-done.18), channel_id=1, source_target_pairs={{0,4},{4,0},{8,12},{12,8},{16,20},{20,16},{24,28},{28,24},{1,5},{5... | collective-permute-start | bytes 3145736 | tf_op jit(solution)/shard_map/ppermute | solution.py:34
  556.2 24.4 %collective-permute-start.87 = (bf16[256,2048]{1,0:T(8,128)(2,1)S(1)}, bf16[256,2048]{1,0:T(8,128)(2,1)S(1)}, u32[]{:S(2)}, u32[]{:S(2)}) collective-permute-start(bf16[256,2048]{1,0:T(8,128)(2,1)S(1)} %fusion.55), channel_id=1, source_target_pairs={{0,16},{4,12},{8,24},{12,4},{16,0},{20,28},{24,8},{28,20},{1,17},{... | collective-permute-start | bytes 3145736 | tf_op jit(solution)/shard_map/ppermute | solution.py:38
  558.1 25.7 %collective-permute-start.90 = (bf16[256,2048]{1,0:T(8,128)(2,1)}, bf16[256,2048]{1,0:T(8,128)(2,1)S(1)}, u32[]{:S(2)}, u32[]{:S(2)}) collective-permute-start(bf16[256,2048]{1,0:T(8,128)(2,1)} %get-tuple-element.63), channel_id=1, source_target_pairs={{0,4},{4,0},{8,12},{12,8},{16,20},{20,16},{24,28},{28,24},{1,5},{5... | collective-permute-start | bytes 3145736 | tf_op jit(solution)/shard_map/ppermute | solution.py:34
  578.3 14.8 %collective-permute-start.94 = (bf16[256,2048]{1,0:T(8,128)(2,1)S(1)}, bf16[256,2048]{1,0:T(8,128)(2,1)S(1)}, u32[]{:S(2)}, u32[]{:S(2)}) collective-permute-start(bf16[256,2048]{1,0:T(8,128)(2,1)S(1)} %fusion.52), channel_id=1, source_target_pairs={{0,16},{4,12},{8,24},{12,4},{16,0},{20,28},{24,8},{28,20},{1,17},{... | collective-permute-start | bytes 3145736 | tf_op jit(solution)/shard_map/ppermute | solution.py:38
  580.0 15.7 %collective-permute-start.56 = (bf16[256,1536]{1,0:T(8,128)(2,1)}, bf16[256,1536]{1,0:T(8,128)(2,1)S(1)}, u32[]{:S(2)}, u32[]{:S(2)}) collective-permute-start(bf16[256,1536]{1,0:T(8,128)(2,1)} %get-tuple-element.75), channel_id=1, source_target_pairs={{0,4},{4,0},{8,12},{12,8},{16,20},{20,16},{24,28},{28,24},{1,5},{5... | collective-permute-start | bytes 2359304 | tf_op jit(solution)/shard_map/ppermute | solution.py:34
  580.0 16.0 %collective-permute-start.55 = (bf16[256,1536]{1,0:T(8,128)(2,1)}, bf16[256,1536]{1,0:T(8,128)(2,1)S(1)}, u32[]{:S(2)}, u32[]{:S(2)}) collective-permute-start(bf16[256,1536]{1,0:T(8,128)(2,1)} %get-tuple-element.76), channel_id=1, source_target_pairs={{0,4},{4,0},{8,12},{12,8},{16,20},{20,16},{24,28},{28,24},{1,5},{5... | collective-permute-start | bytes 2359304 | tf_op jit(solution)/shard_map/ppermute | solution.py:34
  580.5 25.2 %collective-permute-start.59 = (bf16[256,1536]{1,0:T(8,128)(2,1)S(1)}, bf16[256,1536]{1,0:T(8,128)(2,1)}, u32[]{:S(2)}, u32[]{:S(2)}) collective-permute-start(bf16[256,1536]{1,0:T(8,128)(2,1)S(1)} %fusion.67), channel_id=1, source_target_pairs={{0,16},{4,12},{8,24},{12,4},{16,0},{20,28},{24,8},{28,20},{1,17},{... | collective-permute-start | bytes 2359304 | tf_op jit(solution)/shard_map/ppermute | solution.py:38
  583.8 38.4 %collective-permute-start.82 = (bf16[256,2048]{1,0:T(8,128)(2,1)S(1)}, bf16[256,2048]{1,0:T(8,128)(2,1)S(1)}, u32[]{:S(2)}, u32[]{:S(2)}) collective-permute-start(bf16[256,2048]{1,0:T(8,128)(2,1)S(1)} %copy-done.17), channel_id=1, source_target_pairs={{0,4},{4,0},{8,12},{12,8},{16,20},{20,16},{24,28},{28,24},{1,5},{5... | collective-permute-start | bytes 3145736 | tf_op jit(solution)/shard_map/ppermute | solution.py:34
  593.1 27.9 %collective-permute-start.52 = (bf16[256,2048]{1,0:T(8,128)(2,1)S(1)}, bf16[256,2048]{1,0:T(8,128)(2,1)S(1)}, u32[]{:S(2)}, u32[]{:S(2)}) collective-permute-start(bf16[256,2048]{1,0:T(8,128)(2,1)S(1)} %fusion.59), channel_id=1, source_target_pairs={{0,1},{1,2},{2,3},{3,0},{4,5},{5,6},{6,7},{7,4},{8,9},{9,10},{10,1... | collective-permute-start | bytes 3145736 | tf_op jit(solution)/shard_map/ppermute | solution.py:29
  595.7 45.6 %collective-permute-start.46 = (bf16[256,2048]{1,0:T(8,128)(2,1)S(1)}, bf16[256,2048]{1,0:T(8,128)(2,1)S(1)}, u32[]{:S(2)}, u32[]{:S(2)}) collective-permute-start(bf16[256,2048]{1,0:T(8,128)(2,1)S(1)} %fusion.61), channel_id=1, source_target_pairs={{0,1},{1,2},{2,3},{3,0},{4,5},{5,6},{6,7},{7,4},{8,9},{9,10},{10,1... | collective-permute-start | bytes 3145736 | tf_op jit(solution)/shard_map/ppermute | solution.py:29
  596.0 47.8 %collective-permute-start.88 = (bf16[256,2048]{1,0:T(8,128)(2,1)S(1)}, bf16[256,2048]{1,0:T(8,128)(2,1)S(1)}, u32[]{:S(2)}, u32[]{:S(2)}) collective-permute-start(bf16[256,2048]{1,0:T(8,128)(2,1)S(1)} %get-tuple-element.57), channel_id=1, source_target_pairs={{0,8},{4,20},{8,0},{12,28},{16,24},{20,4},{24,16},{28,12},{1,9},{5... | collective-permute-start | bytes 3145736 | tf_op jit(solution)/shard_map/ppermute | solution.py:42
  605.7 39.4 %collective-permute-start.85 = (bf16[256,2048]{1,0:T(8,128)(2,1)S(1)}, bf16[256,2048]{1,0:T(8,128)(2,1)S(1)}, u32[]{:S(2)}, u32[]{:S(2)}) collective-permute-start(bf16[256,2048]{1,0:T(8,128)(2,1)S(1)} %get-tuple-element.56), channel_id=1, source_target_pairs={{0,16},{4,12},{8,24},{12,4},{16,0},{20,28},{24,8},{28,20},{1,17},{... | collective-permute-start | bytes 3145736 | tf_op jit(solution)/shard_map/ppermute | solution.py:38
  621.0 22.9 %collective-permute-start.54 = (bf16[256,1536]{1,0:T(8,128)(2,1)S(1)}, bf16[256,1536]{1,0:T(8,128)(2,1)S(1)}, u32[]{:S(2)}, u32[]{:S(2)}) collective-permute-start(bf16[256,1536]{1,0:T(8,128)(2,1)S(1)} %copy-done.22), channel_id=1, source_target_pairs={{0,4},{4,0},{8,12},{12,8},{16,20},{20,16},{24,28},{28,24},{1,5},{5... | collective-permute-start | bytes 2359304 | tf_op jit(solution)/shard_map/ppermute | solution.py:34
  622.3 26.5 %collective-permute-start.60 = (bf16[256,1536]{1,0:T(8,128)(2,1)S(1)}, bf16[256,1536]{1,0:T(8,128)(2,1)S(1)}, u32[]{:S(2)}, u32[]{:S(2)}) collective-permute-start(bf16[256,1536]{1,0:T(8,128)(2,1)S(1)} %get-tuple-element.72), channel_id=1, source_target_pairs={{0,8},{4,20},{8,0},{12,28},{16,24},{20,4},{24,16},{28,12},{1,9},{5... | collective-permute-start | bytes 2359304 | tf_op jit(solution)/shard_map/ppermute | solution.py:42
  641.3 18.2 %collective-permute-start.57 = (bf16[256,1536]{1,0:T(8,128)(2,1)S(1)}, bf16[256,1536]{1,0:T(8,128)(2,1)S(1)}, u32[]{:S(2)}, u32[]{:S(2)}) collective-permute-start(bf16[256,1536]{1,0:T(8,128)(2,1)S(1)} %get-tuple-element.71), channel_id=1, source_target_pairs={{0,16},{4,12},{8,24},{12,4},{16,0},{20,28},{24,8},{28,20},{1,17},{... | collective-permute-start | bytes 2359304 | tf_op jit(solution)/shard_map/ppermute | solution.py:38
  643.8 17.7 %collective-permute-start.89 = (bf16[256,2048]{1,0:T(8,128)(2,1)S(1)}, bf16[256,2048]{1,0:T(8,128)(2,1)S(1)}, u32[]{:S(2)}, u32[]{:S(2)}) collective-permute-start(bf16[256,2048]{1,0:T(8,128)(2,1)S(1)} %copy-done.16), channel_id=1, source_target_pairs={{0,4},{4,0},{8,12},{12,8},{16,20},{20,16},{24,28},{28,24},{1,5},{5... | collective-permute-start | bytes 3145736 | tf_op jit(solution)/shard_map/ppermute | solution.py:34
  643.9 26.2 %collective-permute-start.95 = (bf16[256,2048]{1,0:T(8,128)(2,1)S(1)}, bf16[256,2048]{1,0:T(8,128)(2,1)S(1)}, u32[]{:S(2)}, u32[]{:S(2)}) collective-permute-start(bf16[256,2048]{1,0:T(8,128)(2,1)S(1)} %get-tuple-element.55), channel_id=1, source_target_pairs={{0,8},{4,20},{8,0},{12,28},{16,24},{20,4},{24,16},{28,12},{1,9},{5... | collective-permute-start | bytes 3145736 | tf_op jit(solution)/shard_map/ppermute | solution.py:42
  645.1 30.6 %collective-permute-start.92 = (bf16[256,2048]{1,0:T(8,128)(2,1)S(1)}, bf16[256,2048]{1,0:T(8,128)(2,1)S(1)}, u32[]{:S(2)}, u32[]{:S(2)}) collective-permute-start(bf16[256,2048]{1,0:T(8,128)(2,1)S(1)} %get-tuple-element.54), channel_id=1, source_target_pairs={{0,16},{4,12},{8,24},{12,4},{16,0},{20,28},{24,8},{28,20},{1,17},{... | collective-permute-start | bytes 3145736 | tf_op jit(solution)/shard_map/ppermute | solution.py:38
  648.7 71.9 %collective-permute-start.53 = (bf16[256,2048]{1,0:T(8,128)(2,1)}, bf16[256,2048]{1,0:T(8,128)(2,1)}, u32[]{:S(2)}, u32[]{:S(2)}) collective-permute-start(bf16[256,2048]{1,0:T(8,128)(2,1)} %fusion.58), channel_id=1, source_target_pairs={{0,1},{1,2},{2,3},{3,0},{4,5},{5,6},{6,7},{7,4},{8,9},{9,10},{10,1... | collective-permute-start | bytes 3145736 | tf_op jit(solution)/shard_map/ppermute | solution.py:29
  659.5 63.6 %collective-permute-start.47 = (bf16[256,2048]{1,0:T(8,128)(2,1)}, bf16[256,2048]{1,0:T(8,128)(2,1)}, u32[]{:S(2)}, u32[]{:S(2)}) collective-permute-start(bf16[256,2048]{1,0:T(8,128)(2,1)} %fusion.60), channel_id=1, source_target_pairs={{0,1},{1,2},{2,3},{3,0},{4,5},{5,6},{6,7},{7,4},{8,9},{9,10},{10,1... | collective-permute-start | bytes 3145736 | tf_op jit(solution)/shard_map/ppermute | solution.py:29
  661.6 42.0 %collective-permute-start.61 = (bf16[64,1536]{1,0:T(8,128)(2,1)S(1)}, bf16[64,1536]{1,0:T(8,128)(2,1)S(1)}, u32[]{:S(2)}, u32[]{:S(2)}) collective-permute-start(bf16[64,1536]{1,0:T(8,128)(2,1)S(1)} %get-tuple-element.90), channel_id=1, source_target_pairs={{0,1},{1,2},{2,3},{3,0},{4,5},{5,6},{6,7},{7,4},{8,9},{9,10},{10,1... | collective-permute-start | bytes 589832 | tf_op jit(solution)/shard_map/ppermute | solution.py:29
  678.9 32.0 %collective-permute-start.62 = (bf16[64,1536]{1,0:T(8,128)(2,1)S(1)}, bf16[64,1536]{1,0:T(8,128)(2,1)S(1)}, u32[]{:S(2)}, u32[]{:S(2)}) collective-permute-start(bf16[64,1536]{1,0:T(8,128)(2,1)S(1)} %get-tuple-element.89), channel_id=1, source_target_pairs={{0,2},{1,3},{2,0},{3,1},{4,6},{5,7},{6,4},{7,5},{8,10},{9,11},{10,... | collective-permute-start | bytes 589832 | tf_op jit(solution)/shard_map/ppermute | solution.py:29
  678.9 32.7 %collective-permute-start.63 = (bf16[64,1536]{1,0:T(8,128)(2,1)S(1)}, bf16[64,1536]{1,0:T(8,128)(2,1)S(1)}, u32[]{:S(2)}, u32[]{:S(2)}) collective-permute-start(bf16[64,1536]{1,0:T(8,128)(2,1)S(1)} %get-tuple-element.88), channel_id=1, source_target_pairs={{0,3},{1,0},{2,1},{3,2},{4,7},{5,4},{6,5},{7,6},{8,11},{9,8},{10,9... | collective-permute-start | bytes 589832 | tf_op jit(solution)/shard_map/ppermute | solution.py:29
  (80 other events, 1463.4 us)
